TPU v7x, 32 devices: a whole 2x2x4 slice. The times are simulated.
32 devices in a mesh: dp: 8 (over z, x), mp: 4 (over y, core).
Axes of the slice: x: 2, y: 2, z: 4, core: 2. Of those that a mesh axis runs over, the one named last changes fastest.
Arguments:
- tokens: bfloat16 [2048, 8192], P('dp', 'mp'), may hold values from -6 to 6
- cotangent: bfloat16 [2048, 8192], P('dp', 'mp'), may hold values from -6 to 6
- w_in: bfloat16 [64, 4, 256, 256], P('mp'), may hold values from -0.1875 to 0.1875
- w_out: bfloat16 [64, 4, 256, 256], P('mp'), may hold values from -0.125 to 0.125
- in_blocks: int32 [64, 4], P('mp'), may hold values from 0 to 31, as said below
- out_blocks: int32 [64, 4], P('mp'), may hold values from 0 to 31, as said below
Outputs:
- output: bfloat16 [2048, 8192], P('dp', 'mp')
- grad_tokens: bfloat16 [2048, 8192], P('dp', 'mp')
- grad_in: float32 [64, 4, 256, 256], P('mp', None, 'dp')
- grad_out: float32 [64, 4, 256, 256], P('mp', None, 'dp')
Inputs may be any that keep to these rules, and one draw needn't show every extreme that they name: `in_blocks`: flat butterfly pattern: row j holds p(j mod 32 XOR m) for m = 0, 1, 2, 4, with p a permutation of the 32 input blocks; the 4 entries of a row differ and every block is named by exactly 8 rows. `out_blocks`: the same flat butterfly form with its own permutation q of the 32 output blocks.
All inputs are finite; a program needn't handle non-finite values.
Results may differ from a plain program's by a relative error of at most 0.018.
Values may be sent and summed in bfloat16 or wider, within the bound.
A program may use at most 128 MiB of HBM per device.

v0:
```python
import functools
import math

import jax
import jax.numpy as jnp
from jax import lax
from jax.experimental import pallas as pl
from jax.experimental.pallas import tpu as pltpu
from jax.sharding import PartitionSpec as P

MB = 2
MASKS = (0, 1, 2, 4)
MESH = pl.DeviceIdType.MESH
C0 = math.sqrt(2.0 / math.pi)
C1 = 0.044715
SKEW = 2


def place_blocks(values, targets, row_blocks):
    step_tok = values.shape[0]
    side = values.shape[-1]
    flat = values.reshape(step_tok, -1, side)
    placed = (
        jnp.zeros((step_tok, row_blocks, side), jnp.float32).at[:, targets.reshape(-1)].add(flat)
    )
    return placed.reshape(step_tok, row_blocks * side)


def shards_plain(tokens, cotangent, w_in, w_out, in_blocks, out_blocks):
    hb_dev, kk, side, _ = w_in.shape
    total_tok = tokens.shape[0]
    width = tokens.shape[1] * lax.axis_size("mp")
    row_blocks = width // side
    passes = MB
    step_tok = total_tok // passes
    grad_in = jnp.zeros(w_in.shape, jnp.float32)
    grad_out = jnp.zeros(w_out.shape, jnp.float32)
    out_share = None
    outputs = []
    backs = []
    for index in range(passes):
        x_part = tokens[index * step_tok : (index + 1) * step_tok]
        dy_part = cotangent[index * step_tok : (index + 1) * step_tok]
        x_full = lax.all_gather(x_part, "mp", axis=1, tiled=True)
        selected = x_full.reshape(step_tok, row_blocks, side)[:, in_blocks]
        pre = jnp.einsum("tjkb,jkbc->tjc", selected, w_in, preferred_element_type=jnp.float32)
        act = jax.nn.gelu(pre).astype(jnp.bfloat16)
        terms = jnp.einsum("tjb,jkbc->tjkc", act, w_out, preferred_element_type=jnp.float32)
        partial_out = place_blocks(terms, out_blocks, row_blocks)
        outputs.append(
            lax.psum_scatter(
                partial_out.astype(jnp.bfloat16), "mp", scatter_dimension=1, tiled=True
            )
        )
        dy_full = lax.all_gather(dy_part, "mp", axis=1, tiled=True)
        picked = dy_full.reshape(step_tok, row_blocks, side)[:, out_blocks]
        d_act = jnp.einsum("tjkc,jkbc->tjb", picked, w_out, preferred_element_type=jnp.float32)
        _, pullback = jax.vjp(jax.nn.gelu, pre)
        d_pre = pullback(d_act)[0].astype(jnp.bfloat16)
        grad_out = grad_out + jnp.einsum(
            "tjb,tjkc->jkbc", act, picked, preferred_element_type=jnp.float32
        )
        grad_in = grad_in + jnp.einsum(
            "tjkb,tjc->jkbc", selected, d_pre, preferred_element_type=jnp.float32
        )
        back = jnp.einsum("tjc,jkbc->tjkb", d_pre, w_in, preferred_element_type=jnp.float32)
        partial_back = place_blocks(back, in_blocks, row_blocks)
        backs.append(
            lax.psum_scatter(
                partial_back.astype(jnp.bfloat16), "mp", scatter_dimension=1, tiled=True
            )
        )
    scale = 1.0 / math.sqrt(total_tok * lax.axis_size("dp"))
    in_share, out_share = (
        lax.psum_scatter(
            grad_in.astype(jnp.bfloat16), "dp", scatter_dimension=2, tiled=True
        ).astype(jnp.float32),
        lax.psum_scatter(
            grad_out.astype(jnp.bfloat16), "dp", scatter_dimension=2, tiled=True
        ).astype(jnp.float32),
    )
    output = jnp.concatenate(outputs, axis=0)
    grad_tokens = jnp.concatenate(backs, axis=0)
    return (output, grad_tokens, in_share * scale, out_share * scale)


def flip(u, m):
    if m == 0:
        return u
    return u + m * (1 - 2 * ((u // m) % 2))


def dot(a, b, dims):
    return lax.dot_general(a, b, (dims, ((), ())), preferred_element_type=jnp.float32)


def fused_kernel(
    dims,
    in_idx, out_idx, in_inv, out_inv, x_hbm, dy_hbm, win_hbm, wout_hbm,
    part_out, part_back, red,
    full, near, mine, theirs, arrived, act, dpre, act2, dpre2, wbuf, acc, csend, crecv, zbuf,
    own_sem, y_send, y_recv, c_send, c_recv, f_send, f_recv,
    x_send, x_recv, y2_send, y2_recv, c2_send, c2_recv, f2_send, f2_recv,
    p_send, p_recv, pl_sem,
    w_sem, g_send, g_recv, up_send, up_recv, dn_send, dn_recv, zl_sem,
    o_send, o_recv,
):
    ndp, nmp, hb, side, own, tok, rows, n1 = dims
    nz = ndp // 2
    dp = lax.axis_index("dp")
    mp = lax.axis_index("mp")
    z, mx = dp // 2, dp % 2
    y, core = mp // 2, mp % 2
    other_core = (dp, y * 2 + 1 - core)
    other_y = (dp, (1 - y) * 2 + core)
    other_x = (z * 2 + 1 - mx, mp)
    above = ((dp + 2) % ndp, mp)
    below = ((dp + ndp - 2) % ndp, mp)
    has_above = z < nz - 1
    has_below = z > 0
    g_core = other_core[1]
    g_y = other_y[1]
    g_far = (1 - y) * 2 + 1 - core
    srcs = (x_hbm, dy_hbm)
    parts = (part_out, part_back)
    nk = len(MASKS)

    barrier = pltpu.get_barrier_semaphore()
    peers = [other_core, other_y, other_x] + [((dp + 2 * dz) % ndp, mp) for dz in range(1, nz)]
    for peer in peers:
        pl.semaphore_signal(barrier, inc=1, device_id=peer, device_id_type=MESH)
    pl.semaphore_wait(barrier, len(peers))

    def remote(src, dst, ssem, rsem, peer):
        return pltpu.make_async_remote_copy(
            src_ref=src, dst_ref=dst, send_sem=ssem, recv_sem=rsem,
            device_id=peer, device_id_type=MESH,
        )

    def lanes(i):
        return pl.ds(pl.multiple_of(i * side, side), side)

    def piece(a, i):
        return srcs[a].at[:, lanes(i)]

    def to_y(a, i, slot):
        return remote(piece(a, i), full.at[a, slot * own + i], y_send.at[a, i], y_recv.at[a, i], other_y)

    def to_core(a, i, slot):
        return remote(piece(a, i), full.at[a, slot * own + i], c_send.at[a, i], c_recv.at[a, i], other_core)

    def forward(a, i, slot):
        return remote(
            full.at[a, g_y * own + i], full.at[a, slot * own + i],
            f_send.at[a, i], f_recv.at[a, i], other_core,
        )

    def to_near(a, i):
        return remote(piece(a, i), near.at[a, mp * own + i], x_send.at[a, i], x_recv.at[a, i], other_x)

    def near_y(a, i, slot):
        return remote(
            near.at[a, mp * own + i], near.at[a, slot * own + i],
            y2_send.at[a, i], y2_recv.at[a, i], other_y,
        )

    def near_core(a, i, slot):
        return remote(
            near.at[a, mp * own + i], near.at[a, slot * own + i],
            c2_send.at[a, i], c2_recv.at[a, i], other_core,
        )

    def near_forward(a, i, slot):
        return remote(
            near.at[a, g_y * own + i], near.at[a, slot * own + i],
            f2_send.at[a, i], f2_recv.at[a, i], other_core,
        )

    def keep(a, i):
        return pltpu.make_async_copy(piece(a, i), full.at[a, mp * own + i], own_sem.at[a, i])

    def w_copies(j, slot):
        return (
            pltpu.make_async_copy(win_hbm.at[j], wbuf.at[slot, 0], w_sem.at[slot, 0, 0]),
            pltpu.make_async_copy(wout_hbm.at[j], wbuf.at[slot, 1], w_sem.at[slot, 1, 0]),
        )

    def loop(n, body, first=0):
        lax.fori_loop(first, n, lambda i, c: (body(i), c)[1], 0)

    for a in range(2):
        def start(i, a=a):
            to_y(a, i, mp).start()
            to_near(a, i).start()
            to_core(a, i, mp).start()
            keep(a, i).start()
        loop(own, start)
    for cp in w_copies(0, 0):
        cp.start()
    for a in range(2):
        def relay(i, a=a):
            to_y(a, i, g_y).wait_recv()
            forward(a, i, g_y).start()
            to_near(a, i).wait_recv()
            near_y(a, i, mp).start()
            near_core(a, i, mp).start()
        loop(own, relay)
    for a in range(2):
        def settle(i, a=a):
            keep(a, i).wait()
            to_core(a, i, g_core).wait_recv()
            forward(a, i, g_far).wait_recv()
        loop(own, settle)

    def hidden_of(source, act_ref, dpre_ref):
        def hidden(j):
            slot = j % 2
            for cp in w_copies(j, slot):
                cp.wait()

            @pl.when(j + 1 < hb)
            def _():
                for cp in w_copies(j + 1, 1 - slot):
                    cp.start()

            pre = jnp.zeros((tok, side), jnp.float32)
            d_act = jnp.zeros((tok, side), jnp.float32)
            for k in range(nk):
                pre += dot(source[0, in_idx[j, k]], wbuf[slot, 0, k], ((1,), (0,)))
                d_act += dot(source[1, out_idx[j, k]], wbuf[slot, 1, k], ((1,), (1,)))
            th = jnp.tanh(C0 * (pre + C1 * (pre * pre * pre)))
            half = 0.5 * (1.0 + th)
            slope = half + 0.5 * pre * (1.0 - th * th) * (C0 * (1.0 + 3.0 * C1 * pre * pre))
            act_ref[j] = (pre * half).astype(jnp.bfloat16)
            dpre_ref[j] = (d_act * slope).astype(jnp.bfloat16)

        loop(hb, hidden)

    hidden_of(full, act, dpre)

    def to_x(j):
        return remote(theirs.at[j], arrived.at[j], g_send.at[j], g_recv.at[j], other_x)

    def split(value):
        value = value.astype(jnp.bfloat16).reshape(nz, 2, rows, side)
        low, high = value[:, 0], value[:, 1]
        return jnp.where(mx == 0, low, high), jnp.where(mx == 0, high, low)

    def weight_grads(j):
        for k in range(nk):
            gi = dot(full[0, in_idx[j, k]], dpre[j], ((0,), (0,)))
            go = dot(act[j], full[1, out_idx[j, k]], ((0,), (0,)))
            for a, value in ((0, gi), (1, go)):
                mine_half, their_half = split(value)
                mine[j, a, k] = mine_half
                theirs[j, a, k] = their_half
        to_x(j).start()

    loop(n1, weight_grads)

    def v_copies(u, slot):
        res = []
        for k, m in enumerate(MASKS):
            v = flip(u, m)
            res.append(pltpu.make_async_copy(win_hbm.at[v, k], wbuf.at[slot, 0, k], w_sem.at[slot, 0, k]))
            res.append(pltpu.make_async_copy(wout_hbm.at[v, k], wbuf.at[slot, 1, k], w_sem.at[slot, 1, k]))
        return res

    for cp in v_copies(0, 0):
        cp.start()

    def place(u):
        slot = u % 2
        for cp in v_copies(u, slot):
            cp.wait()

        @pl.when(u + 1 < hb)
        def _():
            for cp in v_copies(u + 1, 1 - slot):
                cp.start()

        out = jnp.zeros((tok, side), jnp.float32)
        back = jnp.zeros((tok, side), jnp.float32)
        for k, m in enumerate(MASKS):
            v = flip(u, m)
            out += dot(act[v], wbuf[slot, 1, k], ((1,), (0,)))
            back += dot(dpre[v], wbuf[slot, 0, k], ((1,), (1,)))
        acc[0, u] = out.astype(jnp.bfloat16)
        acc[1, u] = back.astype(jnp.bfloat16)

    loop(hb, place)
    for cp in w_copies(0, 0):
        cp.start()
    inv = (out_inv, in_inv)
    for a in range(2):
        acc[a, hb] = jnp.zeros((tok, side), jnp.bfloat16)

    def swap(a):
        return remote(csend.at[a], crecv.at[a], o_send.at[a], o_recv.at[a], other_core)

    for a in range(2):
        for yy in range(2):
            def fill(i, a=a, yy=yy):
                csend[a, yy, i] = acc[a, inv[a][(2 * yy + 1 - core) * own + i]]
            loop(own, fill)
        swap(a).start()

    def to_part(a, i):
        return remote(
            crecv.at[a, 1 - y, i], parts[a].at[1, :, lanes(i)], p_send.at[a, i], p_recv.at[a, i], other_y
        )

    def keep_part(a, i):
        return pltpu.make_async_copy(crecv.at[a, y, i], parts[a].at[0, :, lanes(i)], pl_sem.at[a, i])

    for a in range(2):
        swap(a).wait_recv()
        for yy in range(2):
            def join(i, a=a, yy=yy):
                crecv[a, yy, i] = crecv[a, yy, i] + acc[a, inv[a][(2 * yy + core) * own + i]]
            loop(own, join)

        def emit(i, a=a):
            to_part(a, i).start()
            keep_part(a, i).start()
        loop(own, emit)

    def up(j, u, last):
        dst = red.at[1, :, j] if last else zbuf.at[u - 1, j]
        return remote(mine.at[j, :, :, u], dst, up_send.at[u - 1, j], up_recv.at[u - 1, j], above)

    def down(j, u, last):
        dst = red.at[2, :, j] if last else zbuf.at[u, j]
        return remote(mine.at[j, :, :, u], dst, dn_send.at[u, j], dn_recv.at[u, j], below)

    def keep_z(j):
        return pltpu.make_async_copy(mine.at[j, :, :, z], red.at[0, :, j], zl_sem.at[j])

    def add_in(j, u, slot):
        for a in range(2):
            mine[j, a, :, u] = (
                mine[j, a, :, u].astype(jnp.float32) + zbuf[slot, j, a].astype(jnp.float32)
            ).astype(jnp.bfloat16)

    def hops(t):
        ju = t - SKEW * z
        jd = t - SKEW * (nz - 1 - z)
        up_ok = jnp.logical_and(ju >= 0, ju < hb)
        dn_ok = jnp.logical_and(jd >= 0, jd < hb)
        for u in range(nz - 1, 0, -1):
            @pl.when(jnp.logical_and(up_ok, z < u))
            def _(u=u):
                @pl.when(has_below)
                def _():
                    up(ju, u, False).wait_recv()
                    add_in(ju, u, u - 1)

                @pl.when(z == u - 1)
                def _():
                    up(ju, u, True).start()

                @pl.when(z < u - 1)
                def _():
                    up(ju, u, False).start()
        for u in range(nz - 1):
            @pl.when(jnp.logical_and(dn_ok, z > u))
            def _(u=u):
                @pl.when(has_above)
                def _():
                    down(jd, u, False).wait_recv()
                    add_in(jd, u, u)

                @pl.when(z == u + 1)
                def _():
                    down(jd, u, True).start()

                @pl.when(z > u + 1)
                def _():
                    down(jd, u, False).start()

    def first_steps(t):
        to_x(t).wait_recv()
        for a in range(2):
            for k in range(nk):
                mine[t, a, k] = (
                    mine[t, a, k].astype(jnp.float32) + arrived[t, a, k].astype(jnp.float32)
                ).astype(jnp.bfloat16)
        keep_z(t).start()
        hops(t)

    loop(n1, first_steps)

    for a in range(2):
        def relay2(i, a=a):
            near_y(a, i, g_y).wait_recv()
            near_forward(a, i, g_y).start()
        loop(own, relay2)
    for a in range(2):
        def settle2(i, a=a):
            near_core(a, i, g_core).wait_recv()
            near_forward(a, i, g_far).wait_recv()
        loop(own, settle2)

    hidden_of(near, act2, dpre2)

    def later_steps(t):
        for k in range(nk):
            gi = dot(full[0, in_idx[t, k]], dpre[t], ((0,), (0,)))
            gi += dot(near[0, in_idx[t, k]], dpre2[t], ((0,), (0,)))
            go = dot(act[t], full[1, out_idx[t, k]], ((0,), (0,)))
            go += dot(act2[t], near[1, out_idx[t, k]], ((0,), (0,)))
            mine[t, 0, k] = split(gi)[0]
            mine[t, 1, k] = split(go)[0]
        keep_z(t).start()
        hops(t)

    loop(hb, later_steps, n1)
    loop(hb + SKEW * (nz - 2), hops, hb)

    for a in range(2):
        def drain(i, a=a):
            to_y(a, i, mp).wait_send()
            to_core(a, i, mp).wait_send()
            forward(a, i, g_y).wait_send()
            to_near(a, i).wait_send()
            near_y(a, i, mp).wait_send()
            near_core(a, i, mp).wait_send()
            near_forward(a, i, g_y).wait_send()
            to_part(a, i).wait_send()
            to_part(a, i).wait_recv()
            keep_part(a, i).wait()
        loop(own, drain)
        swap(a).wait_send()

    def sent(j):
        to_x(j).wait_send()

    loop(n1, sent)

    def finish(j):
        keep_z(j).wait()
        for u in range(1, nz):
            @pl.when(z < u)
            def _(u=u):
                up(j, u, True).wait_send()

            @pl.when(z == u)
            def _(u=u):
                up(j, u, True).wait_recv()
        for u in range(nz - 1):
            @pl.when(z > u)
            def _(u=u):
                down(j, u, True).wait_send()

            @pl.when(z == u)
            def _(u=u):
                down(j, u, True).wait_recv()

    loop(hb, finish)


def shards_fused(ndp, nmp, tokens, cotangent, w_in, w_out, in_blocks, out_blocks):
    hb, kk, side, _ = w_in.shape
    tok, feats = tokens.shape
    own = feats // side
    blocks = own * nmp
    nz = ndp // 2
    rows = side // ndp
    n1 = 3 * hb // 16

    def inverse(table):
        hit = table[:, 0][None, :] == jnp.arange(blocks, dtype=jnp.int32)[:, None]
        where = jnp.sum(jnp.where(hit, jnp.arange(hb, dtype=jnp.int32)[None, :], 0), axis=1)
        return jnp.where(jnp.any(hit, axis=1), where, hb).astype(jnp.int32)

    bf = jnp.bfloat16
    any_spec = pl.BlockSpec(memory_space=pl.ANY)
    smem = pl.BlockSpec(memory_space=pltpu.SMEM)
    dma = pltpu.SemaphoreType.DMA
    part_out, part_back, red = pl.pallas_call(
        functools.partial(fused_kernel, (ndp, nmp, hb, side, own, tok, rows, n1)),
        out_shape=(
            jax.ShapeDtypeStruct((2, tok, feats), bf),
            jax.ShapeDtypeStruct((2, tok, feats), bf),
            jax.ShapeDtypeStruct((3, 2, hb, kk, rows, side), bf),
        ),
        in_specs=[smem] * 4 + [any_spec] * 4,
        out_specs=(any_spec,) * 3,
        scratch_shapes=[
            pltpu.VMEM((2, blocks, tok, side), bf),
            pltpu.VMEM((2, blocks, tok, side), bf),
            pltpu.VMEM((hb, 2, kk, nz, rows, side), bf),
            pltpu.VMEM((n1, 2, kk, nz, rows, side), bf),
            pltpu.VMEM((n1, 2, kk, nz, rows, side), bf),
            pltpu.VMEM((hb, tok, side), bf),
            pltpu.VMEM((hb, tok, side), bf),
            pltpu.VMEM((hb, tok, side), bf),
            pltpu.VMEM((hb, tok, side), bf),
            pltpu.VMEM((2, 2, kk, side, side), bf),
            pltpu.VMEM((2, hb + 1, tok, side), bf),
            pltpu.VMEM((2, 2, own, tok, side), bf),
            pltpu.VMEM((2, 2, own, tok, side), bf),
            pltpu.VMEM((nz - 1, hb, 2, kk, rows, side), bf),
        ]
        + [dma((2, own))] * 18
        + [dma((2, 2, kk)), dma((n1,)), dma((n1,))]
        + [dma((nz - 1, hb))] * 4
        + [dma((hb,))]
        + [dma((2,))] * 2,
        compiler_params=pltpu.CompilerParams(
            collective_id=0, has_side_effects=True, vmem_limit_bytes=67_000_000
        ),
    )(
        in_blocks, out_blocks, inverse(in_blocks), inverse(out_blocks),
        tokens, cotangent, w_in, w_out,
    )
    scale = 1.0 / math.sqrt(tok * ndp)
    wide = jnp.float32
    z = lax.axis_index("dp") // 2

    def both(part):
        return (part[0].astype(wide) + part[1].astype(wide)).astype(bf)

    def total(a):
        low = jnp.where(z > 0, red[1, a].astype(wide), 0.0)
        high = jnp.where(z < nz - 1, red[2, a].astype(wide), 0.0)
        return (red[0, a].astype(wide) + low + high) * scale

    return both(part_out), both(part_back), total(0), total(1)


def solution(mesh):
    ndp, nmp = mesh.shape["dp"], mesh.shape["mp"]

    def shards(tokens, cotangent, w_in, w_out, in_blocks, out_blocks):
        hb, kk, side, _ = w_in.shape
        blocks = tokens.shape[1] * nmp // side
        fits = (
            nmp == 4
            and ndp % 2 == 0
            and ndp > 4
            and kk == len(MASKS)
            and 2 * hb == blocks
            and hb % 8 == 0
            and side % (16 * ndp) == 0
        )
        args = (tokens, cotangent, w_in, w_out, in_blocks, out_blocks)
        if fits:
            return shards_fused(ndp, nmp, *args)
        return shards_plain(*args)

    placed = (
        P("dp", "mp"),
        P("dp", "mp"),
        P("mp", None, None, None),
        P("mp", None, None, None),
        P("mp", None),
        P("mp", None),
    )
    return jax.shard_map(
        shards,
        mesh=mesh,
        in_specs=placed,
        out_specs=(
            P("dp", "mp"),
            P("dp", "mp"),
            P("mp", None, "dp", None),
            P("mp", None, "dp", None),
        ),
        check_vma=False,
    )
```

profile of v0, /device:TPU:0, one launch (start us, length us, event | category | flops | bytes accessed | tf_op | source)
XLA Modules:
  0.0 270.6 jit_solution(6360835204545627048)
XLA Ops:
  0.6 0.7 slice_bitcast_fusion.1
  1.3 0.7 slice_bitcast_fusion
  2.0 0.1 select_reduce_fusion
  2.1 0.1 fusion.2
  2.2 0.5 broadcast_select_fusion.out_inv
  2.7 0.1 select_reduce_fusion.1
  2.8 0.1 fusion.3
  2.9 0.5 broadcast_select_fusion.1.in_inv
  3.4 1.4 copy.12.in_idx
  4.8 1.4 copy.13.out_idx
  6.1 256.4 %shard_map.93 = (bf16[2,256,2048]{2,1,0:T(8,128)(2,1)}, bf16[2,256,2048]{2,1,0:T(8,128)(2,1)}, bf16[3,2,16,4,32,256]{5,4,3,2,1,0:T(8,128)(2,1)}) custom-call(s32[16,4]{1,0:T(8,128)} %copy.12.in_idx, s32[16,4]{1,0:T(8,128)} %copy.13.out_idx, s32[32]{0:T(128)} %broadcast_select_fusion.1.in_inv, s32[32]{0:T(128)} %broadcast_select_fusion.out_inv, ...), custom_call_target="tpu_custom_call" | custom-call | tf_op jit(solution)/shard_map/pallas_call | solution.py:480
  262.5 0.0 copy-start
  262.5 4.5 %fusion = (bf16[256,2048]{1,0:T(8,128)(2,1)}, bf16[256,2048]{1,0:T(8,128)(2,1)}) fusion(bf16[2,256,2048]{2,1,0:T(8,128)(2,1)} %get-tuple-element.7, bf16[2,256,2048]{2,1,0:T(8,128)(2,1)} %get-tuple-element.8), kind=kLoop, calls=%fused_computation.4 | loop fusion | flops 4194304 | bytes 6291456 | tf_op jit(solution)/shard_map/convert_element_type | solution.py:522
  267.0 0.0 copy-done
  267.0 3.5 %multiply_bitcast_fusion = (f32[16,4,32,256]{3,2,1,0:T(8,128)}, f32[16,4,32,256]{3,2,1,0:T(8,128)}) fusion(bf16[3,2,16,4,32,256]{5,4,3,2,1,0:T(8,128)(2,1)S(1)} %copy-done, pred[]{:T(512)S(6)} %lt.4, pred[]{:T(512)S(6)} %gt.4), kind=kLoop, calls=%fused_computation | loop fusion | flops 8388608 | bytes 10485762 | tf_op jit(solution)/shard_map/mul | solution.py:527
Async XLA Ops:
  262.5 4.6 %copy-start = (bf16[3,2,16,4,32,256]{5,4,3,2,1,0:T(8,128)(2,1)S(1)}, bf16[3,2,16,4,32,256]{5,4,3,2,1,0:T(8,128)(2,1)}, u32[]{:S(2)}) copy-start(bf16[3,2,16,4,32,256]{5,4,3,2,1,0:T(8,128)(2,1)} %get-tuple-element.9) | copy-start | bytes 18874372
where the time goes:
time: 272 us; the launch traced here: 271 us
  Pallas kernels  256 us (94%)
  other arithmetic  9.48 us (3%)
  local copies, waits for them, and re-layouts  4.08 us (2%)
    pallas_call x1, Pallas kernels, shards_fused(): pl.pallas_call(functools.partial(fused_kernel, (ndp, nmp, hb, side, own,...  256 us

commit v1 on v0

v1 whole, which is shorter than its diff:
```python
import functools
import math

import jax
import jax.numpy as jnp
from jax import lax
from jax.experimental import pallas as pl
from jax.experimental.pallas import tpu as pltpu
from jax.sharding import PartitionSpec as P

MB = 2
MASKS = (0, 1, 2, 4)
MESH = pl.DeviceIdType.MESH
C0 = math.sqrt(2.0 / math.pi)
C1 = 0.044715
GROUP = 8
NQ = 4
BOTH = 0


def place_blocks(values, targets, row_blocks):
    step_tok = values.shape[0]
    side = values.shape[-1]
    flat = values.reshape(step_tok, -1, side)
    placed = (
        jnp.zeros((step_tok, row_blocks, side), jnp.float32).at[:, targets.reshape(-1)].add(flat)
    )
    return placed.reshape(step_tok, row_blocks * side)


def shards_plain(tokens, cotangent, w_in, w_out, in_blocks, out_blocks):
    hb_dev, kk, side, _ = w_in.shape
    total_tok = tokens.shape[0]
    width = tokens.shape[1] * lax.axis_size("mp")
    row_blocks = width // side
    passes = MB
    step_tok = total_tok // passes
    grad_in = jnp.zeros(w_in.shape, jnp.float32)
    grad_out = jnp.zeros(w_out.shape, jnp.float32)
    out_share = None
    outputs = []
    backs = []
    for index in range(passes):
        x_part = tokens[index * step_tok : (index + 1) * step_tok]
        dy_part = cotangent[index * step_tok : (index + 1) * step_tok]
        x_full = lax.all_gather(x_part, "mp", axis=1, tiled=True)
        selected = x_full.reshape(step_tok, row_blocks, side)[:, in_blocks]
        pre = jnp.einsum("tjkb,jkbc->tjc", selected, w_in, preferred_element_type=jnp.float32)
        act = jax.nn.gelu(pre).astype(jnp.bfloat16)
        terms = jnp.einsum("tjb,jkbc->tjkc", act, w_out, preferred_element_type=jnp.float32)
        partial_out = place_blocks(terms, out_blocks, row_blocks)
        outputs.append(
            lax.psum_scatter(
                partial_out.astype(jnp.bfloat16), "mp", scatter_dimension=1, tiled=True
            )
        )
        dy_full = lax.all_gather(dy_part, "mp", axis=1, tiled=True)
        picked = dy_full.reshape(step_tok, row_blocks, side)[:, out_blocks]
        d_act = jnp.einsum("tjkc,jkbc->tjb", picked, w_out, preferred_element_type=jnp.float32)
        _, pullback = jax.vjp(jax.nn.gelu, pre)
        d_pre = pullback(d_act)[0].astype(jnp.bfloat16)
        grad_out = grad_out + jnp.einsum(
            "tjb,tjkc->jkbc", act, picked, preferred_element_type=jnp.float32
        )
        grad_in = grad_in + jnp.einsum(
            "tjkb,tjc->jkbc", selected, d_pre, preferred_element_type=jnp.float32
        )
        back = jnp.einsum("tjc,jkbc->tjkb", d_pre, w_in, preferred_element_type=jnp.float32)
        partial_back = place_blocks(back, in_blocks, row_blocks)
        backs.append(
            lax.psum_scatter(
                partial_back.astype(jnp.bfloat16), "mp", scatter_dimension=1, tiled=True
            )
        )
    scale = 1.0 / math.sqrt(total_tok * lax.axis_size("dp"))
    in_share, out_share = (
        lax.psum_scatter(
            grad_in.astype(jnp.bfloat16), "dp", scatter_dimension=2, tiled=True
        ).astype(jnp.float32),
        lax.psum_scatter(
            grad_out.astype(jnp.bfloat16), "dp", scatter_dimension=2, tiled=True
        ).astype(jnp.float32),
    )
    output = jnp.concatenate(outputs, axis=0)
    grad_tokens = jnp.concatenate(backs, axis=0)
    return (output, grad_tokens, in_share * scale, out_share * scale)


def flip(u, m):
    if m == 0:
        return u
    return u + m * (1 - 2 * ((u // m) % 2))


def dot(a, b, dims):
    return lax.dot_general(a, b, (dims, ((), ())), preferred_element_type=jnp.float32)


def fused_kernel(dims, idx, x_hbm, dy_hbm, win_hbm, wout_hbm, part_out, part_back, red, *scratch):
    ndp, nmp, hb, side, own, tok, rows = dims
    fulls = scratch[:NQ]
    (
        xg, xall, act, dpre, acth, dpreh, mine, theirs, arrived, wbuf, acc, csend, crecv,
        own_sem, y_send, y_recv, c_send, c_recv, f_send, f_recv,
        z_send, z_recv, b_send, b_recv, yf_send, yf_recv, go_sem, w_sem,
        o_send, o_recv, p_send, p_recv, pl_sem, g_send, g_recv, r_send, r_recv, rl_sem,
    ) = scratch[NQ:]
    nz = ndp // 2
    tc = tok // NQ
    nk = len(MASKS)
    dp = lax.axis_index("dp")
    mp = lax.axis_index("mp")
    z, x = dp // 2, dp % 2
    y, core = mp // 2, mp % 2
    other_core = (dp, y * 2 + 1 - core)
    other_y = (dp, (1 - y) * 2 + core)
    other_x = (z * 2 + 1 - x, mp)
    g_core = other_core[1]
    g_y = other_y[1]
    g_far = (1 - y) * 2 + 1 - core
    heavy = core == z // 2
    hbase = (z % 2) * GROUP
    srcs = (x_hbm, dy_hbm)
    parts = (part_out, part_back)

    barrier = pltpu.get_barrier_semaphore()
    peers = [other_core, other_y, other_x] + [((dp + 2 * dz) % ndp, mp) for dz in range(1, nz)]
    for peer in peers:
        pl.semaphore_signal(barrier, inc=1, device_id=peer, device_id_type=MESH)
    pl.semaphore_wait(barrier, len(peers))

    def remote(src, dst, ssem, rsem, peer):
        return pltpu.make_async_remote_copy(
            src_ref=src, dst_ref=dst, send_sem=ssem, recv_sem=rsem,
            device_id=peer, device_id_type=MESH,
        )

    def lanes(i):
        return pl.ds(pl.multiple_of(i * side, side), side)

    def rows_at(base, n):
        return pl.ds(pl.multiple_of(base, n), n)

    def held(a, q, slot):
        return fulls[q].at[a, pl.ds(slot * own, own)]

    def piece(a, q, i):
        return srcs[a].at[pl.ds(q * tc, tc), lanes(i)]

    def to_y(a, q, src, dst):
        return remote(src, dst, y_send.at[a, q], y_recv.at[a, q], other_y)

    def to_core(a, q, src, dst):
        return remote(src, dst, c_send.at[a, q], c_recv.at[a, q], other_core)

    def keep(a, q, src, dst):
        return pltpu.make_async_copy(src, dst, own_sem.at[a, q])

    def landed(send, a, q, slot):
        return send(a, q, held(a, q, slot), held(a, q, slot))

    def forward(a, q, slot):
        return remote(held(a, q, g_y), held(a, q, slot), f_send.at[a, q], f_recv.at[a, q], other_core)

    def w_copies(j, slot):
        return (
            pltpu.make_async_copy(win_hbm.at[j], wbuf.at[slot, 0], w_sem.at[slot, 0, 0]),
            pltpu.make_async_copy(wout_hbm.at[j], wbuf.at[slot, 1], w_sem.at[slot, 1, 0]),
        )

    def loop(n, body, first=0):
        lax.fori_loop(first, n, lambda i, c: (body(i), c)[1], 0)

    for q in range(NQ):
        for a in range(2):
            def start(i, a=a, q=q):
                src, dst = piece(a, q, i), fulls[q].at[a, mp * own + i]
                to_y(a, q, src, dst).start()
                to_core(a, q, src, dst).start()
                keep(a, q, src, dst).start()

            loop(own, start)
    for cp in w_copies(0, 0):
        cp.start()

    def z_rows(zs, q):
        return rows_at(zs * tok + q * tc, tc)

    def z_main(b, zs, q):
        return remote(
            xg.at[y, pl.ds(b * GROUP, GROUP), pl.ds(q * tc, tc)],
            xall.at[y, :, z_rows(zs, q)],
            z_send.at[b, q], z_recv.at[zs, q], ((2 * core + b) * 2 + x, mp),
        )

    def z_both(b, zs, q):
        return remote(
            xg.at[1 - y, pl.ds(b * GROUP, BOTH), pl.ds(q * tc, tc)],
            xall.at[1 - y, pl.ds(0, BOTH), z_rows(zs, q)],
            b_send.at[b, q], b_recv.at[zs, q], ((2 * core + b) * 2 + x, mp),
        )

    def y_forward(a, zs, q):
        part = xall.at[a, pl.ds(BOTH, GROUP - BOTH), z_rows(zs, q)]
        return remote(part, part, yf_send.at[zs, q], yf_recv.at[zs, q], other_y)

    def pass_on(q):
        @pl.when(heavy)
        def _():
            for dz in range(1, nz):
                zs = (z + dz) % nz
                z_main(0, zs, q).wait_recv()
                y_forward(y, zs, q).start()

    for q in range(NQ):
        for a in range(2):
            landed(to_y, a, q, g_y).wait_recv()
            forward(a, q, g_y).start()
        for a in range(2):
            landed(keep, a, q, mp).wait()
            landed(to_core, a, q, g_core).wait_recv()
            forward(a, q, g_far).wait_recv()

        def pack(i, q=q):
            for a in range(2):
                xg[a, i, pl.ds(q * tc, tc)] = fulls[q][a, idx[a, i]]

        loop(hb, pack)
        for b in range(2):
            @pl.when(2 * core + b != z)
            def _(b=b, q=q):
                z_main(b, z, q).start()
                if BOTH:
                    z_both(b, z, q).start()

        @pl.when(heavy)
        def _(q=q):
            def own_rows(r):
                for a in range(2):
                    xall[a, r, z_rows(z, q)] = xg[a, hbase + r, pl.ds(q * tc, tc)]

            loop(GROUP, own_rows)

        if q:
            pass_on(q - 1)

    def hidden_math(source_in, source_out, slot):
        pre = dot(source_in(0), wbuf[slot, 0, 0], ((1,), (0,)))
        d_act = dot(source_out(0), wbuf[slot, 1, 0], ((1,), (1,)))
        for k in range(1, nk):
            pre += dot(source_in(k), wbuf[slot, 0, k], ((1,), (0,)))
            d_act += dot(source_out(k), wbuf[slot, 1, k], ((1,), (1,)))
        th = jnp.tanh(C0 * (pre + C1 * (pre * pre * pre)))
        half = 0.5 * (1.0 + th)
        slope = half + 0.5 * pre * (1.0 - th * th) * (C0 * (1.0 + 3.0 * C1 * pre * pre))
        return (pre * half).astype(jnp.bfloat16), (d_act * slope).astype(jnp.bfloat16)

    def hidden(j):
        slot = j % 2
        for cp in w_copies(j, slot):
            cp.wait()

        @pl.when(j + 1 < hb)
        def _():
            for cp in w_copies(j + 1, 1 - slot):
                cp.start()

        act[j], dpre[j] = hidden_math(
            lambda k: xg[0, flip(j, MASKS[k])], lambda k: xg[1, flip(j, MASKS[k])], slot
        )

    loop(hb, hidden)
    pass_on(NQ - 1)

    def v_copies(u, slot):
        res = []
        for k, m in enumerate(MASKS):
            v = flip(u, m)
            res.append(pltpu.make_async_copy(win_hbm.at[v, k], wbuf.at[slot, 0, k], w_sem.at[slot, 0, k]))
            res.append(pltpu.make_async_copy(wout_hbm.at[v, k], wbuf.at[slot, 1, k], w_sem.at[slot, 1, k]))
        return res

    for cp in v_copies(0, 0):
        cp.start()

    @pl.when(heavy)
    def _():
        def own_hidden(r):
            acth[r, rows_at(z * tok, tok)] = act[hbase + r]
            dpreh[r, rows_at(z * tok, tok)] = dpre[hbase + r]

        loop(GROUP, own_hidden)

    def place(u):
        slot = u % 2
        for cp in v_copies(u, slot):
            cp.wait()

        @pl.when(u + 1 < hb)
        def _():
            for cp in v_copies(u + 1, 1 - slot):
                cp.start()

        out = jnp.zeros((tok, side), jnp.float32)
        back = jnp.zeros((tok, side), jnp.float32)
        for k, m in enumerate(MASKS):
            v = flip(u, m)
            out += dot(act[v], wbuf[slot, 1, k], ((1,), (0,)))
            back += dot(dpre[v], wbuf[slot, 0, k], ((1,), (1,)))
        acc[0, u] = out.astype(jnp.bfloat16)
        acc[1, u] = back.astype(jnp.bfloat16)

    loop(hb, place)
    for a in range(2):
        acc[a, hb] = jnp.zeros((tok, side), jnp.bfloat16)

    @pl.when(heavy)
    def _():
        for cp in w_copies(hbase, 0):
            cp.start()

    tables = (1, 0)

    def swap(a):
        return remote(csend.at[a], crecv.at[a], o_send.at[a], o_recv.at[a], other_core)

    for a in range(2):
        for yy in range(2):
            def fill(i, a=a, yy=yy):
                csend[a, yy, i] = acc[a, idx[tables[a], hb + (2 * yy + 1 - core) * own + i]]
            loop(own, fill)
        swap(a).start()

    def to_part(a, i):
        return remote(
            crecv.at[a, 1 - y, i], parts[a].at[1, :, lanes(i)], p_send.at[a, i], p_recv.at[a, i], other_y
        )

    def keep_part(a, i):
        return pltpu.make_async_copy(crecv.at[a, y, i], parts[a].at[0, :, lanes(i)], pl_sem.at[a, i])

    for a in range(2):
        swap(a).wait_recv()
        for yy in range(2):
            def join(i, a=a, yy=yy):
                crecv[a, yy, i] = crecv[a, yy, i] + acc[a, idx[tables[a], hb + (2 * yy + core) * own + i]]
            loop(own, join)

    @pl.when(heavy)
    def _():
        for q in range(NQ):
            for dz in range(1, nz):
                zs = (z + dz) % nz
                y_forward(1 - y, zs, q).wait_recv()
                if BOTH:
                    z_both(0, zs, q).wait_recv()
        pl.semaphore_signal(go_sem, inc=1, device_id=other_core, device_id_type=MESH)

    @pl.when(jnp.logical_not(heavy))
    def _():
        pl.semaphore_wait(go_sem, 1)

    for a in range(2):
        def emit(i, a=a):
            to_part(a, i).start()
            keep_part(a, i).start()
        loop(own, emit)

    def to_x(r):
        return remote(theirs.at[r], arrived.at[r], g_send.at[r], g_recv.at[r], other_x)

    def to_z(r, zd, b, zs):
        return remote(
            mine.at[r, :, :, zd], red.at[:, b * GROUP + r],
            r_send.at[r, zd], r_recv.at[b, r], (zd * 2 + x, mp),
        )

    def keep_z(r):
        return pltpu.make_async_copy(mine.at[r, :, :, z], red.at[:, hbase + r], rl_sem.at[r])

    def settle(r):
        to_x(r).wait_recv()
        for a in range(2):
            for k in range(nk):
                mine[r, a, k] = (
                    mine[r, a, k].astype(jnp.float32) + arrived[r, a, k].astype(jnp.float32)
                ).astype(jnp.bfloat16)
        for dz in (2, 1, 3):
            to_z(r, (z + dz) % nz, z % 2, z).start()
        keep_z(r).start()

    @pl.when(heavy)
    def _():
        def near_hidden(r):
            slot = r % 2
            for cp in w_copies(hbase + r, slot):
                cp.wait()

            @pl.when(r + 1 < GROUP)
            def _():
                for cp in w_copies(hbase + r + 1, 1 - slot):
                    cp.start()

            def one(dz):
                at = rows_at(((z + dz) % nz) * tok, tok)
                acth[r, at], dpreh[r, at] = hidden_math(
                    lambda k: xall[0, flip(r, MASKS[k]), at], lambda k: xall[1, flip(r, MASKS[k]), at], slot
                )

            loop(nz, one, 1)

        loop(GROUP, near_hidden)

        def grads(r):
            for k, m in enumerate(MASKS):
                gi = dot(xall[0, flip(r, m)], dpreh[r], ((0,), (0,)))
                go = dot(acth[r], xall[1, flip(r, m)], ((0,), (0,)))
                for a, value in ((0, gi), (1, go)):
                    value = value.astype(jnp.bfloat16).reshape(nz, 2, rows, side)
                    low, high = value[:, 0], value[:, 1]
                    mine[r, a, k] = jnp.where(x == 0, low, high)
                    theirs[r, a, k] = jnp.where(x == 0, high, low)
            to_x(r).start()

            @pl.when(r > 0)
            def _():
                settle(r - 1)

        loop(GROUP, grads)
        settle(GROUP - 1)

    for q in range(NQ):
        for a in range(2):
            landed(to_y, a, q, mp).wait_send()
            landed(to_core, a, q, mp).wait_send()
            forward(a, q, g_y).wait_send()
        for b in range(2):
            @pl.when(2 * core + b != z)
            def _(b=b, q=q):
                z_main(b, z, q).wait_send()
                if BOTH:
                    z_both(b, z, q).wait_send()

        @pl.when(heavy)
        def _(q=q):
            for dz in range(1, nz):
                y_forward(y, (z + dz) % nz, q).wait_send()
    for a in range(2):
        def drain(i, a=a):
            to_part(a, i).wait_send()
            to_part(a, i).wait_recv()
            keep_part(a, i).wait()
        loop(own, drain)
        swap(a).wait_send()

    @pl.when(heavy)
    def _():
        def sent(r):
            to_x(r).wait_send()
            keep_z(r).wait()
            for dz in range(1, nz):
                to_z(r, (z + dz) % nz, 0, z).wait_send()

        loop(GROUP, sent)

    for b in range(2):
        @pl.when(2 * core + b != z)
        def _(b=b):
            def got(r):
                to_z(r, z, b, z).wait_recv()

            loop(GROUP, got)


def shards_fused(ndp, nmp, tokens, cotangent, w_in, w_out, in_blocks, out_blocks):
    hb, kk, side, _ = w_in.shape
    tok, feats = tokens.shape
    own = feats // side
    blocks = own * nmp
    nz = ndp // 2
    rows = side // ndp
    tc = tok // NQ
    first = jnp.stack([in_blocks[:, 0], out_blocks[:, 0]])
    place = jnp.arange(hb, dtype=jnp.int32)[:, None]
    hit = first[:, :, None] == jnp.arange(blocks, dtype=jnp.int32)
    table = jnp.concatenate([first, jnp.min(jnp.where(hit, place, hb), axis=1)], axis=1)
    bf = jnp.bfloat16
    any_spec = pl.BlockSpec(memory_space=pl.ANY)
    smem = pl.BlockSpec(memory_space=pltpu.SMEM)
    dma = pltpu.SemaphoreType.DMA
    part_out, part_back, red = pl.pallas_call(
        functools.partial(fused_kernel, (ndp, nmp, hb, side, own, tok, rows)),
        out_shape=(
            jax.ShapeDtypeStruct((2, tok, feats), bf),
            jax.ShapeDtypeStruct((2, tok, feats), bf),
            jax.ShapeDtypeStruct((2, hb, kk, rows, side), bf),
        ),
        in_specs=[smem] + [any_spec] * 4,
        out_specs=(any_spec,) * 3,
        scratch_shapes=[pltpu.VMEM((2, blocks, tc, side), bf)] * NQ
        + [
            pltpu.VMEM((2, hb, tok, side), bf),
            pltpu.VMEM((2, GROUP, nz * tok, side), bf),
            pltpu.VMEM((hb, tok, side), bf),
            pltpu.VMEM((hb, tok, side), bf),
            pltpu.VMEM((GROUP, nz * tok, side), bf),
            pltpu.VMEM((GROUP, nz * tok, side), bf),
            pltpu.VMEM((GROUP, 2, kk, nz, rows, side), bf),
            pltpu.VMEM((GROUP, 2, kk, nz, rows, side), bf),
            pltpu.VMEM((GROUP, 2, kk, nz, rows, side), bf),
            pltpu.VMEM((2, 2, kk, side, side), bf),
            pltpu.VMEM((2, hb + 1, tok, side), bf),
            pltpu.VMEM((2, 2, own, tok, side), bf),
            pltpu.VMEM((2, 2, own, tok, side), bf),
        ]
        + [dma((2, NQ))] * 7
        + [dma((2, NQ)), dma((nz, NQ))] * 2
        + [dma((nz, NQ))] * 2
        + [pltpu.SemaphoreType.REGULAR, dma((2, 2, kk))]
        + [dma((2,))] * 2
        + [dma((2, own))] * 3
        + [dma((GROUP,))] * 2
        + [dma((GROUP, nz)), dma((2, GROUP)), dma((GROUP,))],
        compiler_params=pltpu.CompilerParams(
            collective_id=0, has_side_effects=True, vmem_limit_bytes=67_000_000
        ),
    )(
        table,
        tokens, cotangent, w_in, w_out,
    )
    scale = 1.0 / math.sqrt(tok * ndp)
    wide = jnp.float32

    def both(part):
        return (part[0].astype(wide) + part[1].astype(wide)).astype(bf)

    return both(part_out), both(part_back), red[0].astype(wide) * scale, red[1].astype(wide) * scale


def solution(mesh):
    ndp, nmp = mesh.shape["dp"], mesh.shape["mp"]

    def shards(tokens, cotangent, w_in, w_out, in_blocks, out_blocks):
        hb, kk, side, _ = w_in.shape
        blocks = tokens.shape[1] * nmp // side
        fits = (
            nmp == 4
            and kk == len(MASKS)
            and ndp == 2 * nmp
            and blocks == GROUP * nmp
            and 2 * hb == blocks
            and tokens.shape[0] % (16 * NQ) == 0
            and side % (16 * ndp) == 0
        )
        args = (tokens, cotangent, w_in, w_out, in_blocks, out_blocks)
        if fits:
            return shards_fused(ndp, nmp, *args)
        return shards_plain(*args)

    placed = (
        P("dp", "mp"),
        P("dp", "mp"),
        P("mp", None, None, None),
        P("mp", None, None, None),
        P("mp", None),
        P("mp", None),
    )
    return jax.shard_map(
        shards,
        mesh=mesh,
        in_specs=placed,
        out_specs=(
            P("dp", "mp"),
            P("dp", "mp"),
            P("mp", None, "dp", None),
            P("mp", None, "dp", None),
        ),
        check_vma=False,
    )
```

time: 272 us -> 184 us (0.68)
  Pallas kernels: 256 us -> 173 us
  local copies, waits for them, and re-layouts: 4.08 us -> 1.31 us
    pallas_call x1, Pallas kernels: 256 us -> 173 us  [shards_fused(): pl.pallas_call(functools.partial(fused_kernel, (ndp, nmp, hb, side, own,...]
where the time goes in v1:
time: 184 us; the launch traced here: 183 us
  Pallas kernels  173 us (94%)
  other arithmetic  7.78 us (4%)
    pallas_call x1, Pallas kernels, shards_fused(): pl.pallas_call(functools.partial(fused_kernel, (ndp, nmp, hb, side, own,...  173 us
    convert_element_type x2, other arithmetic, both(): return (part[0].astype(wide) + part[1].astype(wide)).astype(bf)  4.42 us

profile of v1, /device:TPU:0, one launch (start us, length us, event | category | flops | bytes accessed | tf_op | source)
XLA Modules:
  0.0 183.1 jit_solution(13596849662541593835)
XLA Ops:
  0.6 0.7 slice_bitcast_fusion
  1.3 0.1 select_reduce_fusion
  1.4 0.6 pad_add_fusion.1.idx
  2.1 173.4 %shard_map.93 = (bf16[2,256,2048]{2,1,0:T(8,128)(2,1)}, bf16[2,256,2048]{2,1,0:T(8,128)(2,1)}, bf16[2,16,4,32,256]{4,3,2,1,0:T(8,128)(2,1)}) custom-call(s32[2,48]{1,0:T(2,128)} %pad_add_fusion.1.idx, bf16[256,2048]{1,0:T(8,128)(2,1)} %x_hbm.1, bf16[256,2048]{1,0:T(8,128)(2,1)} %dy_hbm.1, bf16[16,4,256,256]{3,2,1,0:T(8,128)(2,1)} %win_hbm.1, ...), custom_call_target="tpu_custom_call" | custom-call | tf_op jit(solution)/shard_map/pallas_call | solution.py:491
  175.5 0.0 copy-start.1
  175.5 3.1 %fusion = bf16[256,2048]{1,0:T(8,128)(2,1)} fusion(bf16[2,256,2048]{2,1,0:T(8,128)(2,1)} %get-tuple-element.7), kind=kLoop, calls=%fused_computation.4 | loop fusion | flops 2097152 | bytes 3145728 | tf_op jit(solution)/shard_map/convert_element_type | solution.py:535
  178.5 0.0 copy-done.1
  178.5 0.0 copy-start
  178.5 1.4 fusion.1
  179.9 0.6 copy-done
  180.5 2.6 %multiply_bitcast_fusion = (f32[16,4,32,256]{3,2,1,0:T(8,128)}, f32[16,4,32,256]{3,2,1,0:T(8,128)}) fusion(bf16[2,16,4,32,256]{4,3,2,1,0:T(8,128)(2,1)S(1)} %copy-done), kind=kLoop, calls=%fused_computation | loop fusion | flops 2097152 | bytes 6291456 | tf_op jit(solution)/shard_map/mul | solution.py:537
  (1 shorter events, 0.0 us)
Async XLA Ops:
  175.5 3.1 %copy-start.1 = (bf16[2,256,2048]{2,1,0:T(8,128)(2,1)S(1)}, bf16[2,256,2048]{2,1,0:T(8,128)(2,1)}, u32[]{:S(2)}) copy-start(bf16[2,256,2048]{2,1,0:T(8,128)(2,1)} %get-tuple-element.8) | copy-start | bytes 6291460
  178.5 2.0 %copy-start = (bf16[2,16,4,32,256]{4,3,2,1,0:T(8,128)(2,1)S(1)}, bf16[2,16,4,32,256]{4,3,2,1,0:T(8,128)(2,1)}, u32[]{:S(2)}) copy-start(bf16[2,16,4,32,256]{4,3,2,1,0:T(8,128)(2,1)} %get-tuple-element.9) | copy-start | bytes 6291460

commit v2 on v1

v2 whole, which is shorter than its diff:
```python
import functools
import math

import jax
import jax.numpy as jnp
from jax import lax
from jax.experimental import pallas as pl
from jax.experimental.pallas import tpu as pltpu
from jax.sharding import PartitionSpec as P

MB = 2
MASKS = (0, 1, 2, 4)
MESH = pl.DeviceIdType.MESH
C0 = math.sqrt(2.0 / math.pi)
C1 = 0.044715
GROUP = 8
NQ = 4
BOTH = 2
SLOTS = 4


def place_blocks(values, targets, row_blocks):
    step_tok = values.shape[0]
    side = values.shape[-1]
    flat = values.reshape(step_tok, -1, side)
    placed = (
        jnp.zeros((step_tok, row_blocks, side), jnp.float32).at[:, targets.reshape(-1)].add(flat)
    )
    return placed.reshape(step_tok, row_blocks * side)


def shards_plain(tokens, cotangent, w_in, w_out, in_blocks, out_blocks):
    hb_dev, kk, side, _ = w_in.shape
    total_tok = tokens.shape[0]
    width = tokens.shape[1] * lax.axis_size("mp")
    row_blocks = width // side
    passes = MB
    step_tok = total_tok // passes
    grad_in = jnp.zeros(w_in.shape, jnp.float32)
    grad_out = jnp.zeros(w_out.shape, jnp.float32)
    out_share = None
    outputs = []
    backs = []
    for index in range(passes):
        x_part = tokens[index * step_tok : (index + 1) * step_tok]
        dy_part = cotangent[index * step_tok : (index + 1) * step_tok]
        x_full = lax.all_gather(x_part, "mp", axis=1, tiled=True)
        selected = x_full.reshape(step_tok, row_blocks, side)[:, in_blocks]
        pre = jnp.einsum("tjkb,jkbc->tjc", selected, w_in, preferred_element_type=jnp.float32)
        act = jax.nn.gelu(pre).astype(jnp.bfloat16)
        terms = jnp.einsum("tjb,jkbc->tjkc", act, w_out, preferred_element_type=jnp.float32)
        partial_out = place_blocks(terms, out_blocks, row_blocks)
        outputs.append(
            lax.psum_scatter(
                partial_out.astype(jnp.bfloat16), "mp", scatter_dimension=1, tiled=True
            )
        )
        dy_full = lax.all_gather(dy_part, "mp", axis=1, tiled=True)
        picked = dy_full.reshape(step_tok, row_blocks, side)[:, out_blocks]
        d_act = jnp.einsum("tjkc,jkbc->tjb", picked, w_out, preferred_element_type=jnp.float32)
        _, pullback = jax.vjp(jax.nn.gelu, pre)
        d_pre = pullback(d_act)[0].astype(jnp.bfloat16)
        grad_out = grad_out + jnp.einsum(
            "tjb,tjkc->jkbc", act, picked, preferred_element_type=jnp.float32
        )
        grad_in = grad_in + jnp.einsum(
            "tjkb,tjc->jkbc", selected, d_pre, preferred_element_type=jnp.float32
        )
        back = jnp.einsum("tjc,jkbc->tjkb", d_pre, w_in, preferred_element_type=jnp.float32)
        partial_back = place_blocks(back, in_blocks, row_blocks)
        backs.append(
            lax.psum_scatter(
                partial_back.astype(jnp.bfloat16), "mp", scatter_dimension=1, tiled=True
            )
        )
    scale = 1.0 / math.sqrt(total_tok * lax.axis_size("dp"))
    in_share, out_share = (
        lax.psum_scatter(
            grad_in.astype(jnp.bfloat16), "dp", scatter_dimension=2, tiled=True
        ).astype(jnp.float32),
        lax.psum_scatter(
            grad_out.astype(jnp.bfloat16), "dp", scatter_dimension=2, tiled=True
        ).astype(jnp.float32),
    )
    output = jnp.concatenate(outputs, axis=0)
    grad_tokens = jnp.concatenate(backs, axis=0)
    return (output, grad_tokens, in_share * scale, out_share * scale)


def flip(u, m):
    if m == 0:
        return u
    return u + m * (1 - 2 * ((u // m) % 2))


def dot(a, b, dims):
    return lax.dot_general(a, b, (dims, ((), ())), preferred_element_type=jnp.float32)


def fused_kernel(dims, idx, x_hbm, dy_hbm, win_hbm, wout_hbm, part_out, part_back, red, *scratch):
    ndp, nmp, hb, side, own, tok, rows = dims
    fulls = [scratch[a * NQ : (a + 1) * NQ] for a in range(2)]
    (
        xg, xall, act, dpre, acth, dpreh, mine, theirs, arrived, wall, crecv,
        own_sem, y_send, y_recv, c_send, c_recv, f_send, f_recv, z_send, b_send, z_recv, b_recv,
        yf_send, yf_recv, go_sem, w_sem,
        o_send, o_recv, p_send, p_recv, pl_sem, g_send, g_recv, r_send, r_recv, rl_sem,
    ) = scratch[2 * NQ :]
    nz = ndp // 2
    tc = tok // NQ
    blocks = own * nmp
    dp = lax.axis_index("dp")
    mp = lax.axis_index("mp")
    z, x = dp // 2, dp % 2
    y, core = mp // 2, mp % 2
    other_core = (dp, y * 2 + 1 - core)
    other_y = (dp, (1 - y) * 2 + core)
    other_x = (z * 2 + 1 - x, mp)
    g_core = other_core[1]
    g_y = other_y[1]
    g_far = (1 - y) * 2 + 1 - core
    heavy = core == z // 2
    hbase = (z % 2) * GROUP
    srcs = (x_hbm, dy_hbm)
    parts = (part_out, part_back)

    barrier = pltpu.get_barrier_semaphore()
    peers = [other_core, other_y, other_x] + [((dp + 2 * dz) % ndp, mp) for dz in range(1, nz)]
    for peer in peers:
        pl.semaphore_signal(barrier, inc=1, device_id=peer, device_id_type=MESH)
    pl.semaphore_wait(barrier, len(peers))

    def remote(src, dst, ssem, rsem, peer):
        return pltpu.make_async_remote_copy(
            src_ref=src, dst_ref=dst, send_sem=ssem, recv_sem=rsem,
            device_id=peer, device_id_type=MESH,
        )

    def lanes(i):
        return pl.ds(pl.multiple_of(i * side, side), side)

    def rows_at(base, n):
        return pl.ds(pl.multiple_of(base, tc), n)

    def held(a, q, slot):
        return fulls[a][q].at[pl.ds(slot * own, own)]

    def piece(a, q, i):
        return srcs[a].at[pl.ds(q * tc, tc), lanes(i)]

    def to_y(a, q, src, dst):
        return remote(src, dst, y_send.at[a, q], y_recv.at[a, q], other_y)

    def to_core(a, q, src, dst):
        return remote(src, dst, c_send.at[a, q], c_recv.at[a, q], other_core)

    def keep(a, q, src, dst):
        return pltpu.make_async_copy(src, dst, own_sem.at[a, q])

    def landed(send, a, q, slot):
        return send(a, q, held(a, q, slot), held(a, q, slot))

    def forward(a, q, slot):
        return remote(held(a, q, g_y), held(a, q, slot), f_send.at[a, q], f_recv.at[a, q], other_core)

    def weights(j):
        return (
            pltpu.make_async_copy(win_hbm.at[j], wall.at[0, j], w_sem.at[0, j]),
            pltpu.make_async_copy(wout_hbm.at[j], wall.at[1, j], w_sem.at[1, j]),
        )

    def loop(n, body, first=0):
        lax.fori_loop(first, n, lambda i, c: (body(i), c)[1], 0)

    for first in (True, False):
        for q in range(NQ):
            for a in range(2):
                def start(i, a=a, q=q):
                    src, dst = piece(a, q, i), fulls[a][q].at[mp * own + i]
                    to_y(a, q, src, dst).start()
                    to_core(a, q, src, dst).start()
                    keep(a, q, src, dst).start()

                @pl.when((y != a) if first else (y == a))
                def _(start=start):
                    loop(own, start)

    def fetch(j):
        for cp in weights(j):
            cp.start()

    loop(hb, fetch)

    def z_rows(slot, q):
        return rows_at((q * nz + slot) * tc, tc)

    def z_main(b, slot, q):
        return remote(
            xg.at[y, pl.ds(b * GROUP, GROUP), pl.ds(q * tc, tc)],
            xall.at[y, :, z_rows(slot, q)],
            z_send.at[b, q], z_recv.at[slot, q], ((2 * core + b) * 2 + x, mp),
        )

    def z_both(b, slot, q):
        return remote(
            xg.at[1 - y, pl.ds(b * GROUP, BOTH), pl.ds(q * tc, tc)],
            xall.at[1 - y, pl.ds(0, BOTH), z_rows(slot, q)],
            b_send.at[b, q], b_recv.at[slot, q], ((2 * core + b) * 2 + x, mp),
        )

    def y_forward(a, slot, q):
        part = xall.at[a, pl.ds(BOTH, GROUP - BOTH), z_rows(slot, q)]
        return remote(part, part, yf_send.at[slot, q], yf_recv.at[slot, q], other_y)

    def to_groups(send, q):
        for b in range(2):
            @pl.when(2 * core + b != z)
            def _(b=b):
                send(b, (z - 2 * core - b + nz) % nz, q).start()

    def pass_on(q):
        @pl.when(heavy)
        def _():
            for slot in range(1, nz):
                z_main(0, slot, q).wait_recv()
                y_forward(y, slot, q).start()

    def gather(a, q):
        landed(to_y, a, q, g_y).wait_recv()
        forward(a, q, g_y).start()
        landed(keep, a, q, mp).wait()
        landed(to_core, a, q, g_core).wait_recv()
        forward(a, q, g_far).wait_recv()

        def pack(i):
            xg[a, i, pl.ds(q * tc, tc)] = fulls[a][q][idx[a, i]]

        loop(hb, pack)

        @pl.when(heavy)
        def _():
            def own_rows(r):
                xall[a, r, z_rows(0, q)] = xg[a, hbase + r, pl.ds(q * tc, tc)]

            loop(GROUP, own_rows)

    def hidden_math(xs, dys, j):
        wi = wall[0, j].reshape(len(MASKS) * side, side)
        wo = jnp.concatenate([wall[1, j, k] for k in range(len(MASKS))], axis=1)
        pre = dot(jnp.concatenate(xs, axis=1), wi, ((1,), (0,)))
        d_act = dot(jnp.concatenate(dys, axis=1), wo, ((1,), (1,)))
        sq = pre * pre
        th = jnp.tanh(pre * (C0 + (C0 * C1) * sq))
        half = 0.5 + 0.5 * th
        value = pre * half
        slope = half + value * (1.0 - th) * (C0 + (3.0 * C0 * C1) * sq)
        return value.astype(jnp.bfloat16), (d_act * slope).astype(jnp.bfloat16)

    def hidden(q):
        at = pl.ds(q * tc, tc)

        def one(j):
            if q == 0:
                for cp in weights(j):
                    cp.wait()
            act[j, at], dpre[j, at] = hidden_math(
                [xg[0, flip(j, m), at] for m in MASKS], [xg[1, flip(j, m), at] for m in MASKS], j
            )

        loop(hb, one)

    for q in range(NQ):
        for a in range(2):
            @pl.when(y == a)
            def _(a=a, q=q):
                gather(a, q)

        to_groups(z_main, q)
    for q in range(NQ):
        for a in range(2):
            @pl.when(y != a)
            def _(a=a, q=q):
                gather(a, q)

        if BOTH:
            to_groups(z_both, q)
        if q:
            pass_on(q - 1)
        hidden(q)
    pass_on(NQ - 1)

    for q in range(NQ):
        for a in range(2):
            forward(a, q, g_y).wait_send()
            fulls[a][q][blocks] = jnp.zeros((tc, side), jnp.bfloat16)

    def place(u):
        vs = [flip(u, m) for m in MASKS]
        wo = jnp.concatenate([wall[1, v, k] for k, v in enumerate(vs)], axis=0)
        wi = jnp.concatenate([wall[0, v, k] for k, v in enumerate(vs)], axis=1)
        out = dot(jnp.concatenate([act[v] for v in vs], axis=1), wo, ((1,), (0,)))
        back = dot(jnp.concatenate([dpre[v] for v in vs], axis=1), wi, ((1,), (1,)))
        for a, value in ((0, out), (1, back)):
            value = value.astype(jnp.bfloat16)
            for q in range(NQ):
                fulls[a][q][u] = value[q * tc : (q + 1) * tc]

    loop(hb, place)
    tables = (1, 0)

    def swap(a, q):
        return remote(
            fulls[a][q].at[pl.ds(hb, hb)], crecv.at[a, :, pl.ds(q * tc, tc)],
            o_send.at[a, q], o_recv.at[a, q], other_core,
        )

    for a in range(2):
        for q in range(NQ):
            for yy in range(2):
                def fill(i, a=a, yy=yy, q=q):
                    fulls[a][q][hb + yy * own + i] = fulls[a][q][
                        idx[tables[a], hb + (2 * yy + 1 - core) * own + i]
                    ]
                loop(own, fill)
            swap(a, q).start()

    def to_part(a, i):
        return remote(
            crecv.at[a, (1 - y) * own + i], parts[a].at[1, :, lanes(i)],
            p_send.at[a, i], p_recv.at[a, i], other_y,
        )

    def keep_part(a, i):
        return pltpu.make_async_copy(
            crecv.at[a, y * own + i], parts[a].at[0, :, lanes(i)], pl_sem.at[a, i]
        )

    for a in range(2):
        for q in range(NQ):
            swap(a, q).wait_recv()
            at = pl.ds(q * tc, tc)
            for yy in range(2):
                def join(i, a=a, yy=yy, q=q, at=at):
                    crecv[a, yy * own + i, at] = crecv[a, yy * own + i, at] + fulls[a][q][
                        idx[tables[a], hb + (2 * yy + core) * own + i]
                    ]
                loop(own, join)

    def near(q):
        for slot in range(1, nz):
            y_forward(1 - y, slot, q).wait_recv()
            if BOTH:
                z_both(0, slot, q).wait_recv()
        at = pl.ds((q * nz + 1) * tc, (nz - 1) * tc)

        def one(r):
            acth[r, at], dpreh[r, at] = hidden_math(
                [xall[0, flip(r, m), at] for m in MASKS], [xall[1, flip(r, m), at] for m in MASKS], hbase + r
            )

        loop(GROUP, one)

    @pl.when(heavy)
    def _():
        def own_hidden(r):
            for q in range(NQ):
                acth[r, z_rows(0, q)] = act[hbase + r, pl.ds(q * tc, tc)]
                dpreh[r, z_rows(0, q)] = dpre[hbase + r, pl.ds(q * tc, tc)]

        loop(GROUP, own_hidden)
        for q in range(NQ):
            near(q)
        pl.semaphore_signal(go_sem, inc=1, device_id=other_core, device_id_type=MESH)

    @pl.when(jnp.logical_not(heavy))
    def _():
        pl.semaphore_wait(go_sem, 1)

    for a in range(2):
        def emit(i, a=a):
            to_part(a, i).start()
            keep_part(a, i).start()
        loop(own, emit)

    def to_x(r, a):
        return remote(
            theirs.at[r % SLOTS, a], arrived.at[r, a], g_send.at[r, a], g_recv.at[r, a], other_x
        )

    def to_z(r, a, zd, b):
        return remote(
            mine.at[r, a, :, zd], red.at[a, b * GROUP + r],
            r_send.at[r, a, zd], r_recv.at[b, r, a], (zd * 2 + x, mp),
        )

    def keep_z(r, a):
        return pltpu.make_async_copy(mine.at[r, a, :, z], red.at[a, hbase + r], rl_sem.at[r, a])

    def settle(r, a):
        to_x(r, a).wait_recv()
        mine[r, a] = (
            mine[r, a].astype(jnp.float32) + arrived[r, a].astype(jnp.float32)
        ).astype(jnp.bfloat16)
        for dz in (2, 1, 3):
            to_z(r, a, (z + dz) % nz, z % 2).start()
        keep_z(r, a).start()

    @pl.when(heavy)
    def _():
        def grads(r):
            for a in range(2):
                @pl.when(r >= SLOTS)
                def _(a=a):
                    to_x(r - SLOTS, a).wait_send()

                for k, m in enumerate(MASKS):
                    if a == 0:
                        value = dot(xall[0, flip(r, m)], dpreh[r], ((0,), (0,)))
                    else:
                        value = dot(acth[r], xall[1, flip(r, m)], ((0,), (0,)))
                    value = value.astype(jnp.bfloat16).reshape(nz, 2, rows, side)
                    low, high = value[:, 0], value[:, 1]
                    mine[r, a, k] = jnp.where(x == 0, low, high)
                    theirs[r % SLOTS, a, k] = jnp.where(x == 0, high, low)
                to_x(r, a).start()
                if a == 0:
                    @pl.when(r > 0)
                    def _():
                        settle(r - 1, 1)
                else:
                    settle(r, 0)

        loop(GROUP, grads)
        settle(GROUP - 1, 1)

    for q in range(NQ):
        for a in range(2):
            landed(to_y, a, q, mp).wait_send()
            landed(to_core, a, q, mp).wait_send()
            swap(a, q).wait_send()
        for b in range(2):
            @pl.when(2 * core + b != z)
            def _(b=b, q=q):
                z_main(b, 0, q).wait_send()
                if BOTH:
                    z_both(b, 0, q).wait_send()

        @pl.when(heavy)
        def _(q=q):
            for slot in range(1, nz):
                y_forward(y, slot, q).wait_send()
    for a in range(2):
        def drain(i, a=a):
            to_part(a, i).wait_send()
            to_part(a, i).wait_recv()
            keep_part(a, i).wait()
        loop(own, drain)

    @pl.when(heavy)
    def _():
        def sent(r):
            for a in range(2):
                @pl.when(r >= GROUP - SLOTS)
                def _(a=a):
                    to_x(r, a).wait_send()

                keep_z(r, a).wait()
                for dz in range(1, nz):
                    to_z(r, a, (z + dz) % nz, 0).wait_send()

        loop(GROUP, sent)

    for b in range(2):
        @pl.when(2 * core + b != z)
        def _(b=b):
            def got(r):
                for a in range(2):
                    to_z(r, a, z, b).wait_recv()

            loop(GROUP, got)


def shards_fused(ndp, nmp, tokens, cotangent, w_in, w_out, in_blocks, out_blocks):
    hb, kk, side, _ = w_in.shape
    tok, feats = tokens.shape
    own = feats // side
    blocks = own * nmp
    nz = ndp // 2
    rows = side // ndp
    tc = tok // NQ
    first = jnp.stack([in_blocks[:, 0], out_blocks[:, 0]])
    place = jnp.arange(hb, dtype=jnp.int32)[:, None]
    hit = first[:, :, None] == jnp.arange(blocks, dtype=jnp.int32)
    table = jnp.concatenate([first, jnp.min(jnp.where(hit, place, blocks), axis=1)], axis=1)
    bf = jnp.bfloat16
    any_spec = pl.BlockSpec(memory_space=pl.ANY)
    smem = pl.BlockSpec(memory_space=pltpu.SMEM)
    dma = pltpu.SemaphoreType.DMA
    part_out, part_back, red = pl.pallas_call(
        functools.partial(fused_kernel, (ndp, nmp, hb, side, own, tok, rows)),
        out_shape=(
            jax.ShapeDtypeStruct((2, tok, feats), bf),
            jax.ShapeDtypeStruct((2, tok, feats), bf),
            jax.ShapeDtypeStruct((2, hb, kk, rows, side), bf),
        ),
        in_specs=[smem] + [any_spec] * 4,
        out_specs=(any_spec,) * 3,
        scratch_shapes=[pltpu.VMEM((blocks + 1, tc, side), bf)] * (2 * NQ)
        + [
            pltpu.VMEM((2, hb, tok, side), bf),
            pltpu.VMEM((2, GROUP, nz * tok, side), bf),
            pltpu.VMEM((hb, tok, side), bf),
            pltpu.VMEM((hb, tok, side), bf),
            pltpu.VMEM((GROUP, nz * tok, side), bf),
            pltpu.VMEM((GROUP, nz * tok, side), bf),
            pltpu.VMEM((GROUP, 2, kk, nz, rows, side), bf),
            pltpu.VMEM((SLOTS, 2, kk, nz, rows, side), bf),
            pltpu.VMEM((GROUP, 2, kk, nz, rows, side), bf),
            pltpu.VMEM((2, hb, kk, side, side), bf),
            pltpu.VMEM((2, hb, tok, side), bf),
        ]
        + [dma((2, NQ))] * 9
        + [dma((nz, NQ))] * 4
        + [pltpu.SemaphoreType.REGULAR, dma((2, hb))]
        + [dma((2, NQ))] * 2
        + [dma((2, own))] * 3
        + [dma((GROUP, 2))] * 2
        + [dma((GROUP, 2, nz)), dma((2, GROUP, 2)), dma((GROUP, 2))],
        compiler_params=pltpu.CompilerParams(
            collective_id=0, has_side_effects=True, vmem_limit_bytes=67_000_000
        ),
    )(
        table,
        tokens, cotangent, w_in, w_out,
    )
    scale = 1.0 / math.sqrt(tok * ndp)
    wide = jnp.float32

    def both(part):
        return (part[0].astype(wide) + part[1].astype(wide)).astype(bf)

    return both(part_out), both(part_back), red[0].astype(wide) * scale, red[1].astype(wide) * scale


def solution(mesh):
    ndp, nmp = mesh.shape["dp"], mesh.shape["mp"]

    def shards(tokens, cotangent, w_in, w_out, in_blocks, out_blocks):
        hb, kk, side, _ = w_in.shape
        blocks = tokens.shape[1] * nmp // side
        fits = (
            nmp == 4
            and kk == len(MASKS)
            and ndp == 2 * nmp
            and blocks == GROUP * nmp
            and 2 * hb == blocks
            and tokens.shape[0] % (16 * NQ) == 0
            and side % (16 * ndp) == 0
        )
        args = (tokens, cotangent, w_in, w_out, in_blocks, out_blocks)
        if fits:
            return shards_fused(ndp, nmp, *args)
        return shards_plain(*args)

    placed = (
        P("dp", "mp"),
        P("dp", "mp"),
        P("mp", None, None, None),
        P("mp", None, None, None),
        P("mp", None),
        P("mp", None),
    )
    return jax.shard_map(
        shards,
        mesh=mesh,
        in_specs=placed,
        out_specs=(
            P("dp", "mp"),
            P("dp", "mp"),
            P("mp", None, "dp", None),
            P("mp", None, "dp", None),
        ),
        check_vma=False,
    )
```

time: 184 us -> 164 us (0.89)
  Pallas kernels: 173 us -> 154 us
    pallas_call x1, Pallas kernels: 173 us -> 154 us  [shards_fused(): pl.pallas_call(functools.partial(fused_kernel, (ndp, nmp, hb, side, own,...]
where the time goes in v2:
time: 164 us; the launch traced here: 163 us
  Pallas kernels  154 us (94%)
  other arithmetic  7.78 us (5%)
    pallas_call x1, Pallas kernels, shards_fused(): pl.pallas_call(functools.partial(fused_kernel, (ndp, nmp, hb, side, own,...  154 us
    convert_element_type x2, other arithmetic, both(): return (part[0].astype(wide) + part[1].astype(wide)).astype(bf)  4.42 us

profile of v2, /device:TPU:0, one launch (start us, length us, event | category | flops | bytes accessed | tf_op | source)
XLA Modules:
  0.0 163.5 jit_solution(11034599353413377152)
XLA Ops:
  0.6 0.7 slice_bitcast_fusion
  1.3 0.1 select_reduce_fusion
  1.4 0.6 pad_add_fusion.1.idx
  2.1 153.8 %shard_map.93 = (bf16[2,256,2048]{2,1,0:T(8,128)(2,1)}, bf16[2,256,2048]{2,1,0:T(8,128)(2,1)}, bf16[2,16,4,32,256]{4,3,2,1,0:T(8,128)(2,1)}) custom-call(s32[2,48]{1,0:T(2,128)} %pad_add_fusion.1.idx, bf16[256,2048]{1,0:T(8,128)(2,1)} %x_hbm.1, bf16[256,2048]{1,0:T(8,128)(2,1)} %dy_hbm.1, bf16[16,4,256,256]{3,2,1,0:T(8,128)(2,1)} %win_hbm.1, ...), custom_call_target="tpu_custom_call" | custom-call | tf_op jit(solution)/shard_map/pallas_call | solution.py:499
  155.8 0.0 copy-start.1
  155.8 3.1 %fusion = bf16[256,2048]{1,0:T(8,128)(2,1)} fusion(bf16[2,256,2048]{2,1,0:T(8,128)(2,1)} %get-tuple-element.7), kind=kLoop, calls=%fused_computation.4 | loop fusion | flops 2097152 | bytes 3145728 | tf_op jit(solution)/shard_map/convert_element_type | solution.py:540
  158.9 0.0 copy-done.1
  158.9 0.0 copy-start
  158.9 1.4 fusion.1
  160.3 0.6 copy-done
  160.9 2.6 %multiply_bitcast_fusion = (f32[16,4,32,256]{3,2,1,0:T(8,128)}, f32[16,4,32,256]{3,2,1,0:T(8,128)}) fusion(bf16[2,16,4,32,256]{4,3,2,1,0:T(8,128)(2,1)S(1)} %copy-done), kind=kLoop, calls=%fused_computation | loop fusion | flops 2097152 | bytes 6291456 | tf_op jit(solution)/shard_map/mul | solution.py:542
  (1 shorter events, 0.0 us)
Async XLA Ops:
  155.8 3.1 %copy-start.1 = (bf16[2,256,2048]{2,1,0:T(8,128)(2,1)S(1)}, bf16[2,256,2048]{2,1,0:T(8,128)(2,1)}, u32[]{:S(2)}) copy-start(bf16[2,256,2048]{2,1,0:T(8,128)(2,1)} %get-tuple-element.8) | copy-start | bytes 6291460
  158.9 2.0 %copy-start = (bf16[2,16,4,32,256]{4,3,2,1,0:T(8,128)(2,1)S(1)}, bf16[2,16,4,32,256]{4,3,2,1,0:T(8,128)(2,1)}, u32[]{:S(2)}) copy-start(bf16[2,16,4,32,256]{4,3,2,1,0:T(8,128)(2,1)} %get-tuple-element.9) | copy-start | bytes 6291460

commit v3 on v2

--- a/solution.py
+++ b/solution.py
@@ -15,8 +15,9 @@
 C1 = 0.044715
 GROUP = 8
 NQ = 4
-BOTH = 2
+BOTHS = (3, 3, 2, 2)
 SLOTS = 4
+HALVES = 2
 
 
 def place_blocks(values, targets, row_blocks):
@@ -97,14 +98,14 @@
     return lax.dot_general(a, b, (dims, ((), ())), preferred_element_type=jnp.float32)
 
 
-def fused_kernel(dims, idx, x_hbm, dy_hbm, win_hbm, wout_hbm, part_out, part_back, red, *scratch):
+def fused_kernel(dims, idx, x_hbm, dy_hbm, win_hbm, wout_hbm, out_hbm, back_hbm, red, *scratch):
     ndp, nmp, hb, side, own, tok, rows = dims
     fulls = [scratch[a * NQ : (a + 1) * NQ] for a in range(2)]
     (
         xg, xall, act, dpre, acth, dpreh, mine, theirs, arrived, wall, crecv,
         own_sem, y_send, y_recv, c_send, c_recv, f_send, f_recv, z_send, b_send, z_recv, b_recv,
         yf_send, yf_recv, go_sem, w_sem,
-        o_send, o_recv, p_send, p_recv, pl_sem, g_send, g_recv, r_send, r_recv, rl_sem,
+        free_sem, o_send, o_recv, p_send, p_recv, out_sem, g_send, g_recv, r_send, r_recv, rl_sem,
     ) = scratch[2 * NQ :]
     nz = ndp // 2
     tc = tok // NQ
@@ -122,7 +123,7 @@
     heavy = core == z // 2
     hbase = (z % 2) * GROUP
     srcs = (x_hbm, dy_hbm)
-    parts = (part_out, part_back)
+    outs = (out_hbm, back_hbm)
 
     barrier = pltpu.get_barrier_semaphore()
     peers = [other_core, other_y, other_x] + [((dp + 2 * dz) % ndp, mp) for dz in range(1, nz)]
@@ -163,33 +164,46 @@
     def forward(a, q, slot):
         return remote(held(a, q, g_y), held(a, q, slot), f_send.at[a, q], f_recv.at[a, q], other_core)
 
-    def weights(j):
+    def weights():
         return (
-            pltpu.make_async_copy(win_hbm.at[j], wall.at[0, j], w_sem.at[0, j]),
-            pltpu.make_async_copy(wout_hbm.at[j], wall.at[1, j], w_sem.at[1, j]),
+            pltpu.make_async_copy(win_hbm, wall.at[0], w_sem.at[0]),
+            pltpu.make_async_copy(wout_hbm, wall.at[1], w_sem.at[1]),
         )
 
     def loop(n, body, first=0):
         lax.fori_loop(first, n, lambda i, c: (body(i), c)[1], 0)
 
-    for first in (True, False):
+    def hold(a, q):
+        def start(i):
+            keep(a, q, piece(a, q, i), fulls[a][q].at[mp * own + i]).start()
+
+        loop(own, start)
+
+    def send_first(a):
+        def start(i):
+            to_y(a, 0, piece(a, 0, i), fulls[a][0].at[mp * own + i]).start()
+
+        loop(own, start)
+
+    def send_all(a, lead):
+        if lead:
+            send_first(a)
         for q in range(NQ):
-            for a in range(2):
-                def start(i, a=a, q=q):
-                    src, dst = piece(a, q, i), fulls[a][q].at[mp * own + i]
-                    to_y(a, q, src, dst).start()
-                    to_core(a, q, src, dst).start()
-                    keep(a, q, src, dst).start()
-
-                @pl.when((y != a) if first else (y == a))
-                def _(start=start):
-                    loop(own, start)
-
-    def fetch(j):
-        for cp in weights(j):
-            cp.start()
-
-    loop(hb, fetch)
+            hold(a, q)
+        for q in range(NQ):
+            landed(keep, a, q, mp).wait()
+            if q or not lead:
+                landed(to_y, a, q, mp).start()
+            landed(to_core, a, q, mp).start()
+
+    for a in range(2):
+        @pl.when(y != a)
+        def _(a=a):
+            send_all(a, True)
+            send_all(1 - a, False)
+
+    for cp in weights():
+        cp.start()
 
     def z_rows(slot, q):
         return rows_at((q * nz + slot) * tc, tc)
@@ -198,19 +212,26 @@
         return remote(
             xg.at[y, pl.ds(b * GROUP, GROUP), pl.ds(q * tc, tc)],
             xall.at[y, :, z_rows(slot, q)],
-            z_send.at[b, q], z_recv.at[slot, q], ((2 * core + b) * 2 + x, mp),
+            z_send.at[b, q], z_recv.at[q], ((2 * core + b) * 2 + x, mp),
         )
 
     def z_both(b, slot, q):
         return remote(
-            xg.at[1 - y, pl.ds(b * GROUP, BOTH), pl.ds(q * tc, tc)],
-            xall.at[1 - y, pl.ds(0, BOTH), z_rows(slot, q)],
-            b_send.at[b, q], b_recv.at[slot, q], ((2 * core + b) * 2 + x, mp),
-        )
-
-    def y_forward(a, slot, q):
-        part = xall.at[a, pl.ds(BOTH, GROUP - BOTH), z_rows(slot, q)]
-        return remote(part, part, yf_send.at[slot, q], yf_recv.at[slot, q], other_y)
+            xg.at[1 - y, pl.ds(b * GROUP, BOTHS[q]), pl.ds(q * tc, tc)],
+            xall.at[1 - y, pl.ds(0, BOTHS[q]), z_rows(slot, q)],
+            b_send.at[b, q], b_recv.at[q], ((2 * core + b) * 2 + x, mp),
+        )
+
+    def near_rows(q, first=1):
+        return pl.ds((q * nz + first) * tc, (nz - first) * tc)
+
+    def y_forward(a, q):
+        part = xall.at[a, pl.ds(BOTHS[q], GROUP - BOTHS[q]), near_rows(q)]
+        return remote(part, part, yf_send.at[q], yf_recv.at[q], other_y)
+
+    def z_landed(a, q, n, sem):
+        part = xall.at[a, pl.ds(0, n), near_rows(q)]
+        return remote(part, part, yf_send.at[q], sem.at[q], other_y)
 
     def to_groups(send, q):
         for b in range(2):
@@ -221,14 +242,12 @@
     def pass_on(q):
         @pl.when(heavy)
         def _():
-            for slot in range(1, nz):
-                z_main(0, slot, q).wait_recv()
-                y_forward(y, slot, q).start()
+            z_landed(y, q, GROUP, z_recv).wait_recv()
+            y_forward(y, q).start()
 
     def gather(a, q):
         landed(to_y, a, q, g_y).wait_recv()
         forward(a, q, g_y).start()
-        landed(keep, a, q, mp).wait()
         landed(to_core, a, q, g_core).wait_recv()
         forward(a, q, g_far).wait_recv()
 
@@ -256,18 +275,116 @@
         slope = half + value * (1.0 - th) * (C0 + (3.0 * C0 * C1) * sq)
         return value.astype(jnp.bfloat16), (d_act * slope).astype(jnp.bfloat16)
 
-    def hidden(q):
-        at = pl.ds(q * tc, tc)
+    ht = tok // HALVES
+    per = NQ // HALVES
+
+    def hidden(h, first=0, last=hb):
+        at = pl.ds(h * ht, ht)
 
         def one(j):
-            if q == 0:
-                for cp in weights(j):
-                    cp.wait()
             act[j, at], dpre[j, at] = hidden_math(
                 [xg[0, flip(j, m), at] for m in MASKS], [xg[1, flip(j, m), at] for m in MASKS], j
             )
 
-        loop(hb, one)
+        loop(last, one, first)
+
+    def place(h, u):
+        at = pl.ds(h * ht, ht)
+        vs = [flip(u, m) for m in MASKS]
+        wo = jnp.concatenate([wall[1, v, k] for k, v in enumerate(vs)], axis=0)
+        wi = jnp.concatenate([wall[0, v, k] for k, v in enumerate(vs)], axis=1)
+        out = dot(jnp.concatenate([act[v, at] for v in vs], axis=1), wo, ((1,), (0,)))
+        back = dot(jnp.concatenate([dpre[v, at] for v in vs], axis=1), wi, ((1,), (1,)))
+        for a, value in ((0, out), (1, back)):
+            value = value.astype(jnp.bfloat16)
+            for p in range(per):
+                fulls[a][h * per + p][u] = value[p * tc : (p + 1) * tc]
+
+    tables = (1, 0)
+
+    def swap(a, q):
+        return remote(
+            fulls[a][q].at[pl.ds(hb, hb)], crecv.at[a, :, pl.ds(q * tc, tc)],
+            o_send.at[a, q], o_recv.at[a, q], other_core,
+        )
+
+    def clear(h):
+        for q in range(h * per, (h + 1) * per):
+            for a in range(2):
+                forward(a, q, g_y).wait_send()
+                landed(to_y, a, q, mp).wait_send()
+                landed(to_core, a, q, mp).wait_send()
+                fulls[a][q][blocks] = jnp.zeros((tc, side), jnp.bfloat16)
+
+    def hand_over(h):
+        for a in range(2):
+            for q in range(h * per, (h + 1) * per):
+                for yy in range(2):
+                    def fill(i, a=a, yy=yy, q=q):
+                        fulls[a][q][hb + yy * own + i] = fulls[a][q][
+                            idx[tables[a], hb + (2 * yy + 1 - core) * own + i]
+                        ]
+                    loop(own, fill)
+                swap(a, q).start()
+
+    def to_part(a, h, i):
+        at = pl.ds(h * ht, ht)
+        return remote(
+            crecv.at[a, (1 - y) * own + i, at], xg.at[a, i, at], p_send, p_recv.at[h], other_y
+        )
+
+    def put(a, h, i):
+        at = pl.ds(h * ht, ht)
+        return pltpu.make_async_copy(crecv.at[a, y * own + i, at], outs[a].at[at, lanes(i)], out_sem)
+
+    def finish(h):
+        at = pl.ds(h * ht, ht)
+        part = xg.at[:, pl.ds(0, own), at]
+        remote(part, part, p_send, p_recv.at[h], other_y).wait_recv()
+        for a in range(2):
+            def one(i, a=a):
+                crecv[a, y * own + i, at] = (
+                    crecv[a, y * own + i, at].astype(jnp.float32) + xg[a, i, at].astype(jnp.float32)
+                ).astype(jnp.bfloat16)
+                put(a, h, i).start()
+
+            loop(own, one)
+
+    def merge(h):
+        for a in range(2):
+            for q in range(h * per, (h + 1) * per):
+                swap(a, q).wait_recv()
+                at = pl.ds(q * tc, tc)
+                for yy in range(2):
+                    def join(i, a=a, yy=yy, q=q, at=at):
+                        crecv[a, yy * own + i, at] = crecv[a, yy * own + i, at] + fulls[a][q][
+                            idx[tables[a], hb + (2 * yy + core) * own + i]
+                        ]
+                    loop(own, join)
+
+    def emit(h):
+        pl.semaphore_wait(free_sem.at[h], 1)
+        for a in range(2):
+            loop(own, lambda i, a=a: to_part(a, h, i).start())
+
+    def near(q):
+        y_forward(1 - y, q).wait_recv()
+        if BOTHS[q]:
+            z_landed(1 - y, q, BOTHS[q], b_recv).wait_recv()
+        late = q >= per
+        at = near_rows(q, 0 if late else 1)
+        mine_at, own_at = pl.ds(q * tc, tc), z_rows(0, q)
+
+        def one(r):
+            acth[r, at], dpreh[r, at] = hidden_math(
+                [xall[0, flip(r, m), at] for m in MASKS], [xall[1, flip(r, m), at] for m in MASKS], hbase + r
+            )
+            if late:
+                act[hbase + r, mine_at], dpre[hbase + r, mine_at] = acth[r, own_at], dpreh[r, own_at]
+            else:
+                acth[r, own_at], dpreh[r, own_at] = act[hbase + r, mine_at], dpre[hbase + r, mine_at]
+
+        loop(GROUP, one)
 
     for q in range(NQ):
         for a in range(2):
@@ -276,125 +393,72 @@
                 gather(a, q)
 
         to_groups(z_main, q)
+    for cp in weights():
+        cp.wait()
     for q in range(NQ):
         for a in range(2):
             @pl.when(y != a)
             def _(a=a, q=q):
                 gather(a, q)
 
-        if BOTH:
+        if BOTHS[q]:
             to_groups(z_both, q)
         if q:
             pass_on(q - 1)
-        hidden(q)
+        if q == per - 1:
+            hidden(0)
+            clear(0)
+            loop(hb, lambda u: place(0, u))
+            hand_over(0)
     pass_on(NQ - 1)
-
-    for q in range(NQ):
-        for a in range(2):
-            forward(a, q, g_y).wait_send()
-            fulls[a][q][blocks] = jnp.zeros((tc, side), jnp.bfloat16)
-
-    def place(u):
-        vs = [flip(u, m) for m in MASKS]
-        wo = jnp.concatenate([wall[1, v, k] for k, v in enumerate(vs)], axis=0)
-        wi = jnp.concatenate([wall[0, v, k] for k, v in enumerate(vs)], axis=1)
-        out = dot(jnp.concatenate([act[v] for v in vs], axis=1), wo, ((1,), (0,)))
-        back = dot(jnp.concatenate([dpre[v] for v in vs], axis=1), wi, ((1,), (1,)))
-        for a, value in ((0, out), (1, back)):
-            value = value.astype(jnp.bfloat16)
-            for q in range(NQ):
-                fulls[a][q][u] = value[q * tc : (q + 1) * tc]
-
-    loop(hb, place)
-    tables = (1, 0)
-
-    def swap(a, q):
-        return remote(
-            fulls[a][q].at[pl.ds(hb, hb)], crecv.at[a, :, pl.ds(q * tc, tc)],
-            o_send.at[a, q], o_recv.at[a, q], other_core,
-        )
-
-    for a in range(2):
-        for q in range(NQ):
-            for yy in range(2):
-                def fill(i, a=a, yy=yy, q=q):
-                    fulls[a][q][hb + yy * own + i] = fulls[a][q][
-                        idx[tables[a], hb + (2 * yy + 1 - core) * own + i]
-                    ]
-                loop(own, fill)
-            swap(a, q).start()
-
-    def to_part(a, i):
-        return remote(
-            crecv.at[a, (1 - y) * own + i], parts[a].at[1, :, lanes(i)],
-            p_send.at[a, i], p_recv.at[a, i], other_y,
-        )
-
-    def keep_part(a, i):
-        return pltpu.make_async_copy(
-            crecv.at[a, y * own + i], parts[a].at[0, :, lanes(i)], pl_sem.at[a, i]
-        )
-
-    for a in range(2):
-        for q in range(NQ):
-            swap(a, q).wait_recv()
-            at = pl.ds(q * tc, tc)
-            for yy in range(2):
-                def join(i, a=a, yy=yy, q=q, at=at):
-                    crecv[a, yy * own + i, at] = crecv[a, yy * own + i, at] + fulls[a][q][
-                        idx[tables[a], hb + (2 * yy + core) * own + i]
-                    ]
-                loop(own, join)
-
-    def near(q):
-        for slot in range(1, nz):
-            y_forward(1 - y, slot, q).wait_recv()
-            if BOTH:
-                z_both(0, slot, q).wait_recv()
-        at = pl.ds((q * nz + 1) * tc, (nz - 1) * tc)
-
-        def one(r):
-            acth[r, at], dpreh[r, at] = hidden_math(
-                [xall[0, flip(r, m), at] for m in MASKS], [xall[1, flip(r, m), at] for m in MASKS], hbase + r
-            )
-
-        loop(GROUP, one)
+    merge(0)
+    clear(1)
+
+    def release(h):
+        for q in range(h * per, (h + 1) * per):
+            for b in range(2):
+                @pl.when(2 * core + b != z)
+                def _(b=b, q=q):
+                    z_main(b, 0, q).wait_send()
+                    if BOTHS[q]:
+                        z_both(b, 0, q).wait_send()
+
+        pl.semaphore_signal(free_sem.at[h], inc=1, device_id=other_y, device_id_type=MESH)
 
     @pl.when(heavy)
     def _():
-        def own_hidden(r):
-            for q in range(NQ):
-                acth[r, z_rows(0, q)] = act[hbase + r, pl.ds(q * tc, tc)]
-                dpreh[r, z_rows(0, q)] = dpre[hbase + r, pl.ds(q * tc, tc)]
-
-        loop(GROUP, own_hidden)
-        for q in range(NQ):
+        for q in range(NQ - 1):
             near(q)
+        release(0)
+        near(NQ - 1)
         pl.semaphore_signal(go_sem, inc=1, device_id=other_core, device_id_type=MESH)
+        emit(0)
 
     @pl.when(jnp.logical_not(heavy))
     def _():
+        hidden(1)
+        loop(hb, lambda u: place(1, u))
+        hand_over(1)
+        release(0)
+        release(1)
         pl.semaphore_wait(go_sem, 1)
-
-    for a in range(2):
-        def emit(i, a=a):
-            to_part(a, i).start()
-            keep_part(a, i).start()
-        loop(own, emit)
+        emit(0)
+        merge(1)
+        emit(1)
 
     def to_x(r, a):
         return remote(
-            theirs.at[r % SLOTS, a], arrived.at[r, a], g_send.at[r, a], g_recv.at[r, a], other_x
+            theirs.at[r % SLOTS, a], arrived.at[r, a], g_send.at[r % SLOTS, a], g_recv.at[r, a], other_x
         )
 
     def to_z(r, a, zd, b):
         return remote(
             mine.at[r, a, :, zd], red.at[a, b * GROUP + r],
-            r_send.at[r, a, zd], r_recv.at[b, r, a], (zd * 2 + x, mp),
+            r_send, r_recv.at[b], (zd * 2 + x, mp),
         )
 
     def keep_z(r, a):
-        return pltpu.make_async_copy(mine.at[r, a, :, z], red.at[a, hbase + r], rl_sem.at[r, a])
+        return pltpu.make_async_copy(mine.at[r, a, :, z], red.at[a, hbase + r], rl_sem)
 
     def settle(r, a):
         to_x(r, a).wait_recv()
@@ -407,7 +471,7 @@
 
     @pl.when(heavy)
     def _():
-        def grads(r):
+        def grads(r, stage=2):
             for a in range(2):
                 @pl.when(r >= SLOTS)
                 def _(a=a):
@@ -423,61 +487,62 @@
                     mine[r, a, k] = jnp.where(x == 0, low, high)
                     theirs[r % SLOTS, a, k] = jnp.where(x == 0, high, low)
                 to_x(r, a).start()
-                if a == 0:
-                    @pl.when(r > 0)
-                    def _():
-                        settle(r - 1, 1)
-                else:
-                    settle(r, 0)
-
-        loop(GROUP, grads)
+
+                if stage == 0:
+                    first = GROUP - hbase + a * (GROUP // 2)
+                    hidden(1, first, first + GROUP // 2)
+                if stage == 1:
+                    step = 2 * (r - 1) + a
+                    loop((step + 1) * (hb // 4), lambda u: place(1, u), step * (hb // 4))
+
+                @pl.when(r > 0)
+                def _(a=a):
+                    settle(r - 1, a)
+
+        grads(0, 0)
+        loop(3, functools.partial(grads, stage=1), 1)
+        hand_over(1)
+        release(1)
+        loop(4, grads, 3)
+        merge(1)
+        emit(1)
+        loop(6, grads, 4)
+        finish(0)
+        loop(GROUP, grads, 6)
+        settle(GROUP - 1, 0)
         settle(GROUP - 1, 1)
 
+    @pl.when(jnp.logical_not(heavy))
+    def _():
+        finish(0)
+
+    finish(1)
     for q in range(NQ):
         for a in range(2):
-            landed(to_y, a, q, mp).wait_send()
-            landed(to_core, a, q, mp).wait_send()
             swap(a, q).wait_send()
-        for b in range(2):
-            @pl.when(2 * core + b != z)
-            def _(b=b, q=q):
-                z_main(b, 0, q).wait_send()
-                if BOTH:
-                    z_both(b, 0, q).wait_send()
 
         @pl.when(heavy)
         def _(q=q):
-            for slot in range(1, nz):
-                y_forward(y, slot, q).wait_send()
-    for a in range(2):
-        def drain(i, a=a):
-            to_part(a, i).wait_send()
-            to_part(a, i).wait_recv()
-            keep_part(a, i).wait()
-        loop(own, drain)
+            y_forward(y, q).wait_send()
+
+    remote(crecv.at[0], crecv.at[0], p_send, p_recv.at[0], other_y).wait_send()
+    pltpu.make_async_copy(crecv.at[0], crecv.at[0], out_sem).wait()
 
     @pl.when(heavy)
     def _():
-        def sent(r):
+        for r in range(GROUP - SLOTS, GROUP):
             for a in range(2):
-                @pl.when(r >= GROUP - SLOTS)
-                def _(a=a):
-                    to_x(r, a).wait_send()
-
-                keep_z(r, a).wait()
-                for dz in range(1, nz):
-                    to_z(r, a, (z + dz) % nz, 0).wait_send()
-
-        loop(GROUP, sent)
+                to_x(r, a).wait_send()
+        group = red.at[:, pl.ds(hbase, GROUP)]
+        pltpu.make_async_copy(group, group, rl_sem).wait()
+        sent = mine.at[pl.ds(0, GROUP * (nz - 1) // nz)]
+        remote(sent, sent, r_send, r_recv.at[0], other_x).wait_send()
 
     for b in range(2):
         @pl.when(2 * core + b != z)
         def _(b=b):
-            def got(r):
-                for a in range(2):
-                    to_z(r, a, z, b).wait_recv()
-
-            loop(GROUP, got)
+            got = red.at[:, pl.ds(b * GROUP, GROUP)]
+            remote(got, got, r_send, r_recv.at[b], other_x).wait_recv()
 
 
 def shards_fused(ndp, nmp, tokens, cotangent, w_in, w_out, in_blocks, out_blocks):
@@ -496,11 +561,11 @@
     any_spec = pl.BlockSpec(memory_space=pl.ANY)
     smem = pl.BlockSpec(memory_space=pltpu.SMEM)
     dma = pltpu.SemaphoreType.DMA
-    part_out, part_back, red = pl.pallas_call(
+    output, grad_tokens, red = pl.pallas_call(
         functools.partial(fused_kernel, (ndp, nmp, hb, side, own, tok, rows)),
         out_shape=(
-            jax.ShapeDtypeStruct((2, tok, feats), bf),
-            jax.ShapeDtypeStruct((2, tok, feats), bf),
+            jax.ShapeDtypeStruct((tok, feats), bf),
+            jax.ShapeDtypeStruct((tok, feats), bf),
             jax.ShapeDtypeStruct((2, hb, kk, rows, side), bf),
         ),
         in_specs=[smem] + [any_spec] * 4,
@@ -520,12 +585,12 @@
             pltpu.VMEM((2, hb, tok, side), bf),
         ]
         + [dma((2, NQ))] * 9
-        + [dma((nz, NQ))] * 4
-        + [pltpu.SemaphoreType.REGULAR, dma((2, hb))]
+        + [dma((NQ,))] * 4
+        + [pltpu.SemaphoreType.REGULAR, dma((2,)), pltpu.SemaphoreType.REGULAR((2,))]
         + [dma((2, NQ))] * 2
-        + [dma((2, own))] * 3
-        + [dma((GROUP, 2))] * 2
-        + [dma((GROUP, 2, nz)), dma((2, GROUP, 2)), dma((GROUP, 2))],
+        + [dma, dma((2,)), dma]
+        + [dma((SLOTS, 2)), dma((GROUP, 2))]
+        + [dma, dma((2,)), dma],
         compiler_params=pltpu.CompilerParams(
             collective_id=0, has_side_effects=True, vmem_limit_bytes=67_000_000
         ),
@@ -536,10 +601,7 @@
     scale = 1.0 / math.sqrt(tok * ndp)
     wide = jnp.float32
 
-    def both(part):
-        return (part[0].astype(wide) + part[1].astype(wide)).astype(bf)
-
-    return both(part_out), both(part_back), red[0].astype(wide) * scale, red[1].astype(wide) * scale
+    return output, grad_tokens, red[0].astype(wide) * scale, red[1].astype(wide) * scale
 
 
 def solution(mesh):

time: 164 us -> 150 us (0.915)
  Pallas kernels: 154 us -> 139 us
  other arithmetic: 7.78 us -> 4.99 us
  local copies, waits for them, and re-layouts: 1.31 us -> 3.27 us
    pallas_call x1, Pallas kernels: 154 us -> 139 us  [shards_fused(): pl.pallas_call(functools.partial(fused_kernel, (ndp, nmp, hb, side, own,...]
    convert_element_type x2 -> x0, other arithmetic: 4.42 us -> none  [both(): return (part[0].astype(wide) + part[1].astype(wide)).astype(bf)]
    unnamed x4 -> x6, local copies, waits for them, and re-layouts: 0.61 us -> 2.57 us
where the time goes in v3:
time: 150 us; the launch traced here: 148 us
  Pallas kernels  139 us (93%)
  other arithmetic  4.99 us (3%)
  local copies, waits for them, and re-layouts  3.27 us (2%)
    pallas_call x1, Pallas kernels, shards_fused(): pl.pallas_call(functools.partial(fused_kernel, (ndp, nmp, hb, side, own,...  139 us
    mul x1, other arithmetic, shards_fused(): red[1].astype(wide) * scale  4.25 us

profile of v3, /device:TPU:0, one launch (start us, length us, event | category | flops | bytes accessed | tf_op | source)
XLA Modules:
  0.0 148.3 jit_solution(13533331841914362729)
XLA Ops:
  0.6 0.7 slice_bitcast_fusion
  1.3 0.1 select_reduce_fusion
  1.4 0.6 pad_add_fusion.1.idx
  2.1 139.4 %shard_map.93 = (bf16[256,2048]{1,0:T(8,128)(2,1)}, bf16[256,2048]{1,0:T(8,128)(2,1)}, bf16[2,16,4,32,256]{4,3,2,1,0:T(8,128)(2,1)}) custom-call(s32[2,48]{1,0:T(2,128)} %pad_add_fusion.1.idx, bf16[256,2048]{1,0:T(8,128)(2,1)} %x_hbm.1, bf16[256,2048]{1,0:T(8,128)(2,1)} %dy_hbm.1, bf16[16,4,256,256]{3,2,1,0:T(8,128)(2,1)} %win_hbm.1, ...), custom_call_target="tpu_custom_call" | custom-call | tf_op jit(solution)/shard_map/pallas_call | solution.py:564
  141.5 0.0 copy-start.1
  141.5 4.3 %multiply_bitcast_fusion = (f32[16,4,32,256]{3,2,1,0:T(8,128)}, f32[16,4,32,256]{3,2,1,0:T(8,128)}) fusion(bf16[2,16,4,32,256]{4,3,2,1,0:T(8,128)(2,1)} %get-tuple-element.9), kind=kLoop, calls=%fused_computation | loop fusion | flops 2097152 | bytes 6291456 | tf_op jit(solution)/shard_map/mul | solution.py:604
  145.7 0.0 copy-start
  145.7 0.0 copy-done.1
  145.7 1.0 copy.12
  146.7 0.6 copy-done
  147.3 1.0 copy.13
  (1 shorter events, 0.0 us)
Async XLA Ops:
  141.5 4.3 %copy-start.1 = (bf16[256,2048]{1,0:T(8,128)(2,1)S(1)}, bf16[256,2048]{1,0:T(8,128)(2,1)}, u32[]{:S(2)}) copy-start(bf16[256,2048]{1,0:T(8,128)(2,1)} %get-tuple-element.18) | copy-start | bytes 3145732
  145.7 1.6 %copy-start = (bf16[256,2048]{1,0:T(8,128)(2,1)S(1)}, bf16[256,2048]{1,0:T(8,128)(2,1)}, u32[]{:S(2)}) copy-start(bf16[256,2048]{1,0:T(8,128)(2,1)} %get-tuple-element.19) | copy-start | bytes 3145732

commit v4 on v3

--- a/solution.py
+++ b/solution.py
@@ -15,8 +15,9 @@
 C1 = 0.044715
 GROUP = 8
 NQ = 4
-BOTHS = (3, 3, 2, 2)
+BOTHS = (0, 0, 5, 5)
 SLOTS = 4
+PIECES = 4
 HALVES = 2
 
 
@@ -367,24 +368,22 @@
         for a in range(2):
             loop(own, lambda i, a=a: to_part(a, h, i).start())
 
-    def near(q):
+    def near_landed(q):
         y_forward(1 - y, q).wait_recv()
         if BOTHS[q]:
             z_landed(1 - y, q, BOTHS[q], b_recv).wait_recv()
+
+    def near(q, r):
         late = q >= per
         at = near_rows(q, 0 if late else 1)
         mine_at, own_at = pl.ds(q * tc, tc), z_rows(0, q)
-
-        def one(r):
-            acth[r, at], dpreh[r, at] = hidden_math(
-                [xall[0, flip(r, m), at] for m in MASKS], [xall[1, flip(r, m), at] for m in MASKS], hbase + r
-            )
-            if late:
-                act[hbase + r, mine_at], dpre[hbase + r, mine_at] = acth[r, own_at], dpreh[r, own_at]
-            else:
-                acth[r, own_at], dpreh[r, own_at] = act[hbase + r, mine_at], dpre[hbase + r, mine_at]
-
-        loop(GROUP, one)
+        acth[r, at], dpreh[r, at] = hidden_math(
+            [xall[0, flip(r, m), at] for m in MASKS], [xall[1, flip(r, m), at] for m in MASKS], hbase + r
+        )
+        if late:
+            act[hbase + r, mine_at], dpre[hbase + r, mine_at] = acth[r, own_at], dpreh[r, own_at]
+        else:
+            acth[r, own_at], dpreh[r, own_at] = act[hbase + r, mine_at], dpre[hbase + r, mine_at]
 
     for q in range(NQ):
         for a in range(2):
@@ -427,12 +426,14 @@
 
     @pl.when(heavy)
     def _():
+        release(0)
+        emit(0)
         for q in range(NQ - 1):
-            near(q)
-        release(0)
-        near(NQ - 1)
+            near_landed(q)
+            loop(GROUP, functools.partial(near, q))
+        near_landed(NQ - 1)
         pl.semaphore_signal(go_sem, inc=1, device_id=other_core, device_id_type=MESH)
-        emit(0)
+        near(NQ - 1, 0)
 
     @pl.when(jnp.logical_not(heavy))
     def _():
@@ -471,7 +472,7 @@
 
     @pl.when(heavy)
     def _():
-        def grads(r, stage=2):
+        def grads(r, stage=3):
             for a in range(2):
                 @pl.when(r >= SLOTS)
                 def _(a=a):
@@ -488,11 +489,13 @@
                     theirs[r % SLOTS, a, k] = jnp.where(x == 0, high, low)
                 to_x(r, a).start()
 
-                if stage == 0:
+                if stage == 0 and a == 1:
+                    loop(GROUP, functools.partial(near, NQ - 1), 1)
+                if stage == 1:
                     first = GROUP - hbase + a * (GROUP // 2)
                     hidden(1, first, first + GROUP // 2)
-                if stage == 1:
-                    step = 2 * (r - 1) + a
+                if stage == 2:
+                    step = 2 * (r - 2) + a
                     loop((step + 1) * (hb // 4), lambda u: place(1, u), step * (hb // 4))
 
                 @pl.when(r > 0)
@@ -500,13 +503,14 @@
                     settle(r - 1, a)
 
         grads(0, 0)
-        loop(3, functools.partial(grads, stage=1), 1)
+        grads(1, 1)
+        loop(4, functools.partial(grads, stage=2), 2)
         hand_over(1)
         release(1)
-        loop(4, grads, 3)
+        loop(5, grads, 4)
         merge(1)
         emit(1)
-        loop(6, grads, 4)
+        loop(6, grads, 5)
         finish(0)
         loop(GROUP, grads, 6)
         settle(GROUP - 1, 0)
@@ -543,6 +547,46 @@
         def _(b=b):
             got = red.at[:, pl.ds(b * GROUP, GROUP)]
             remote(got, got, r_send, r_recv.at[b], other_x).wait_recv()
+
+
+def write_kernel(
+    scale, out_hbm, back_hbm, red, out, back, grad_in, grad_out, kept, low, high, k_in, k_out, r_in, r_out
+):
+    n = red.shape[1] // PIECES
+    srcs, dsts, grads = (out_hbm, back_hbm), (out, back), (grad_in, grad_out)
+
+    def load(a, p):
+        at = pl.ds(p * n, n)
+        return pltpu.make_async_copy(red.at[a, at], low.at[a, at], r_in.at[a, p])
+
+    def save(a, p):
+        at = pl.ds(p * n, n)
+        return pltpu.make_async_copy(high.at[a, at], grads[a].at[at], r_out.at[a, p])
+
+    def take(a):
+        return pltpu.make_async_copy(srcs[a], kept.at[a], k_in.at[a])
+
+    def give(a):
+        return pltpu.make_async_copy(kept.at[a], dsts[a], k_out.at[a])
+
+    for p in range(PIECES):
+        for a in range(2):
+            load(a, p).start()
+    for a in range(2):
+        take(a).start()
+    for p in range(PIECES):
+        for a in range(2):
+            load(a, p).wait()
+            at = pl.ds(p * n, n)
+            high[a, at] = low[a, at].astype(jnp.float32) * scale
+            save(a, p).start()
+    for a in range(2):
+        take(a).wait()
+        give(a).start()
+    for a in range(2):
+        for p in range(PIECES):
+            save(a, p).wait()
+        give(a).wait()
 
 
 def shards_fused(ndp, nmp, tokens, cotangent, w_in, w_out, in_blocks, out_blocks):
@@ -600,8 +644,24 @@
     )
     scale = 1.0 / math.sqrt(tok * ndp)
     wide = jnp.float32
-
-    return output, grad_tokens, red[0].astype(wide) * scale, red[1].astype(wide) * scale
+    return pl.pallas_call(
+        functools.partial(write_kernel, scale),
+        out_shape=(
+            jax.ShapeDtypeStruct((tok, feats), bf),
+            jax.ShapeDtypeStruct((tok, feats), bf),
+            jax.ShapeDtypeStruct((hb, kk, rows, side), wide),
+            jax.ShapeDtypeStruct((hb, kk, rows, side), wide),
+        ),
+        in_specs=[any_spec] * 3,
+        out_specs=(any_spec,) * 4,
+        scratch_shapes=[
+            pltpu.VMEM((2, tok, feats), bf),
+            pltpu.VMEM((2, hb, kk, rows, side), bf),
+            pltpu.VMEM((2, hb, kk, rows, side), wide),
+            dma((2,)), dma((2,)), dma((2, PIECES)), dma((2, PIECES)),
+        ],
+        compiler_params=pltpu.CompilerParams(vmem_limit_bytes=67_000_000),
+    )(output, grad_tokens, red)
 
 
 def solution(mesh):

time: 150 us -> 140 us (0.933)
  other arithmetic: 4.99 us -> 0.74 us
  local copies, waits for them, and re-layouts: 3.27 us -> 0.7 us
  Pallas kernels: 139 us -> 137 us
    pallas_call x1, Pallas kernels: 139 us -> 133 us  [shards_fused(): pl.pallas_call(functools.partial(fused_kernel, (ndp, nmp, hb, side, own,...]
    mul x1 -> x0, other arithmetic: 4.25 us -> none  [shards_fused(): red[1].astype(wide) * scale]
    pallas_call x0 -> x1, Pallas kernels: none -> 3.97 us  [shards_fused(): pl.pallas_call(functools.partial(write_kernel, scale), out_shape=(jax.Sha...]
    unnamed x6 -> x0, local copies, waits for them, and re-layouts: 2.57 us -> none
where the time goes in v4:
time: 140 us; the launch traced here: 139 us
  Pallas kernels  137 us (98%)
    pallas_call x1, Pallas kernels, shards_fused(): pl.pallas_call(functools.partial(fused_kernel, (ndp, nmp, hb, side, own,...  133 us
    pallas_call x1, Pallas kernels, shards_fused(): pl.pallas_call(functools.partial(write_kernel, scale), out_shape=(jax.Sha...  3.97 us

profile of v4, /device:TPU:0, one launch (start us, length us, event | category | flops | bytes accessed | tf_op | source)
XLA Modules:
  0.0 139.5 jit_solution(17486910327523118918)
XLA Ops:
  0.6 0.7 slice_bitcast_fusion
  1.3 0.1 select_reduce_fusion
  1.4 0.6 pad_add_fusion.1.idx
  2.1 133.2 %shard_map.93 = (bf16[256,2048]{1,0:T(8,128)(2,1)}, bf16[256,2048]{1,0:T(8,128)(2,1)}, bf16[2,16,4,32,256]{4,3,2,1,0:T(8,128)(2,1)}) custom-call(s32[2,48]{1,0:T(2,128)} %pad_add_fusion.1.idx, bf16[256,2048]{1,0:T(8,128)(2,1)} %x_hbm.1, bf16[256,2048]{1,0:T(8,128)(2,1)} %dy_hbm.1, bf16[16,4,256,256]{3,2,1,0:T(8,128)(2,1)} %win_hbm.1, ...), custom_call_target="tpu_custom_call" | custom-call | tf_op jit(solution)/shard_map/pallas_call | solution.py:608
  135.3 4.0 %shard_map.94 = (bf16[256,2048]{1,0:T(8,128)(2,1)}, bf16[256,2048]{1,0:T(8,128)(2,1)}, f32[16,4,32,256]{3,2,1,0:T(8,128)}, f32[16,4,32,256]{3,2,1,0:T(8,128)}) custom-call(bf16[256,2048]{1,0:T(8,128)(2,1)} %get-tuple-element.7.out_hbm, bf16[256,2048]{1,0:T(8,128)(2,1)} %get-tuple-element.8.back_hbm, bf16[2,16,4,32,256]{4,3,2,1,0:T(8,128)(2,1)} %get-tuple-element.9.red), custom_call_target="tpu_custom_call" | custom-call | tf_op jit(solution)/shard_map/pallas_call | solution.py:647
  (1 shorter events, 0.0 us)

commit v5 on v4

--- a/solution.py
+++ b/solution.py
@@ -15,7 +15,10 @@
 C1 = 0.044715
 GROUP = 8
 NQ = 4
-BOTHS = (0, 0, 5, 5)
+LEAD = ((0, 3), (4, 1))
+REST = ((3, 1), (5, 3))
+RELAY = ((3, 1),)
+BOTH = (5, 3)
 SLOTS = 4
 PIECES = 4
 HALVES = 2
@@ -104,9 +107,9 @@
     fulls = [scratch[a * NQ : (a + 1) * NQ] for a in range(2)]
     (
         xg, xall, act, dpre, acth, dpreh, mine, theirs, arrived, wall, crecv,
-        own_sem, y_send, y_recv, c_send, c_recv, f_send, f_recv, z_send, b_send, z_recv, b_recv,
-        yf_send, yf_recv, go_sem, w_sem,
-        free_sem, o_send, o_recv, p_send, p_recv, out_sem, g_send, g_recv, r_send, r_recv, rl_sem,
+        own_sem, y_send, y_recv, c_send, c_recv, f_send, f_recv, za_send, zb_send, b_send,
+        za_recv, zb_recv, b_recv, fa_send, fa_recv, fb_send, fb_recv, go_sem, w_sem,
+        free_sem, o_send, o_recv, p_send, p_recv, out_sem, g_send, g_recv, x_send, x_recv, r_send, r_recv, rl_sem,
     ) = scratch[2 * NQ :]
     nz = ndp // 2
     tc = tok // NQ
@@ -209,42 +212,45 @@
     def z_rows(slot, q):
         return rows_at((q * nz + slot) * tc, tc)
 
-    def z_main(b, slot, q):
+    def size(spans):
+        return sum(n for _, n in spans)
+
+    def z_span(a, b, slot, q, at, n, ssem, rsem):
         return remote(
-            xg.at[y, pl.ds(b * GROUP, GROUP), pl.ds(q * tc, tc)],
-            xall.at[y, :, z_rows(slot, q)],
-            z_send.at[b, q], z_recv.at[q], ((2 * core + b) * 2 + x, mp),
-        )
-
-    def z_both(b, slot, q):
-        return remote(
-            xg.at[1 - y, pl.ds(b * GROUP, BOTHS[q]), pl.ds(q * tc, tc)],
-            xall.at[1 - y, pl.ds(0, BOTHS[q]), z_rows(slot, q)],
-            b_send.at[b, q], b_recv.at[q], ((2 * core + b) * 2 + x, mp),
+            xg.at[a, pl.ds(b * GROUP + at, n), pl.ds(q * tc, tc)],
+            xall.at[a, pl.ds(at, n), z_rows(slot, q)],
+            ssem.at[b, q], rsem.at[q], ((2 * core + b) * 2 + x, mp),
         )
 
     def near_rows(q, first=1):
         return pl.ds((q * nz + first) * tc, (nz - first) * tc)
 
-    def y_forward(a, q):
-        part = xall.at[a, pl.ds(BOTHS[q], GROUP - BOTHS[q]), near_rows(q)]
-        return remote(part, part, yf_send.at[q], yf_recv.at[q], other_y)
-
-    def z_landed(a, q, n, sem):
-        part = xall.at[a, pl.ds(0, n), near_rows(q)]
-        return remote(part, part, yf_send.at[q], sem.at[q], other_y)
-
-    def to_groups(send, q):
+    def to_groups(a, q, spans, ssem, rsem):
         for b in range(2):
             @pl.when(2 * core + b != z)
             def _(b=b):
-                send(b, (z - 2 * core - b + nz) % nz, q).start()
-
-    def pass_on(q):
+                for at, n in spans:
+                    z_span(a, b, (z - 2 * core - b + nz) % nz, q, at, n, ssem, rsem).start()
+
+    def z_sent(a, b, q, n, ssem, rsem):
+        z_span(a, b, 0, q, 0, n, ssem, rsem).wait_send()
+
+    def near_part(a, q, at, n, ssem, rsem):
+        part = xall.at[a, pl.ds(at, n), near_rows(q)]
+        return remote(part, part, ssem.at[q], rsem.at[q], other_y)
+
+    def pass_on(q, spans, here, ssem, rsem, held_spans):
         @pl.when(heavy)
         def _():
-            z_landed(y, q, GROUP, z_recv).wait_recv()
-            y_forward(y, q).start()
+            near_part(y, q, 0, size(held_spans), ssem, here).wait_recv()
+            for at, n in spans:
+                near_part(y, q, at, n, ssem, rsem).start()
+
+    def pass_lead(q):
+        pass_on(q, LEAD, za_recv, fa_send, fa_recv, LEAD)
+
+    def pass_rest(q):
+        pass_on(q, RELAY, zb_recv, fb_send, fb_recv, REST)
 
     def gather(a, q):
         landed(to_y, a, q, g_y).wait_recv()
@@ -368,77 +374,150 @@
         for a in range(2):
             loop(own, lambda i, a=a: to_part(a, h, i).start())
 
-    def near_landed(q):
-        y_forward(1 - y, q).wait_recv()
-        if BOTHS[q]:
-            z_landed(1 - y, q, BOTHS[q], b_recv).wait_recv()
-
-    def near(q, r):
-        late = q >= per
-        at = near_rows(q, 0 if late else 1)
-        mine_at, own_at = pl.ds(q * tc, tc), z_rows(0, q)
+    def near(r, p):
+        at = pl.ds(pl.multiple_of(p * per * nz * tc, per * nz * tc), per * nz * tc)
         acth[r, at], dpreh[r, at] = hidden_math(
             [xall[0, flip(r, m), at] for m in MASKS], [xall[1, flip(r, m), at] for m in MASKS], hbase + r
         )
-        if late:
-            act[hbase + r, mine_at], dpre[hbase + r, mine_at] = acth[r, own_at], dpreh[r, own_at]
-        else:
-            acth[r, own_at], dpreh[r, own_at] = act[hbase + r, mine_at], dpre[hbase + r, mine_at]
-
-    for q in range(NQ):
-        for a in range(2):
-            @pl.when(y == a)
-            def _(a=a, q=q):
-                gather(a, q)
-
-        to_groups(z_main, q)
-    for cp in weights():
-        cp.wait()
-    for q in range(NQ):
-        for a in range(2):
-            @pl.when(y != a)
-            def _(a=a, q=q):
-                gather(a, q)
-
-        if BOTHS[q]:
-            to_groups(z_both, q)
-        if q:
-            pass_on(q - 1)
-        if q == per - 1:
-            hidden(0)
-            clear(0)
-            loop(hb, lambda u: place(0, u))
-            hand_over(0)
-    pass_on(NQ - 1)
-    merge(0)
-    clear(1)
 
     def release(h):
         for q in range(h * per, (h + 1) * per):
             for b in range(2):
                 @pl.when(2 * core + b != z)
                 def _(b=b, q=q):
-                    z_main(b, 0, q).wait_send()
-                    if BOTHS[q]:
-                        z_both(b, 0, q).wait_send()
+                    z_sent(y, b, q, size(LEAD), za_send, za_recv)
+                    z_sent(y, b, q, size(REST), zb_send, zb_recv)
+                    z_sent(1 - y, b, q, BOTH[1], b_send, b_recv)
 
         pl.semaphore_signal(free_sem.at[h], inc=1, device_id=other_y, device_id_type=MESH)
+
+    for q in range(NQ):
+        for a in range(2):
+            @pl.when(y == a)
+            def _(a=a, q=q):
+                gather(a, q)
+
+        to_groups(y, q, LEAD, za_send, za_recv)
+    for q in range(NQ):
+        to_groups(y, q, REST, zb_send, zb_recv)
+    for cp in weights():
+        cp.wait()
+    for q in range(NQ):
+        for a in range(2):
+            @pl.when(y != a)
+            def _(a=a, q=q):
+                gather(a, q)
+
+        to_groups(1 - y, q, (BOTH,), b_send, b_recv)
+        if q == per - 1:
+            hidden(0)
+        if q == per:
+            pass_lead(0)
+            pass_lead(1)
+            clear(0)
+            loop(hb, lambda u: place(0, u))
+    for q in range(per, NQ):
+        pass_lead(q)
+    hand_over(0)
+    hidden(1)
+    clear(1)
+    merge(0)
+    loop(hb // 2, lambda u: place(1, u))
+    for q in range(NQ):
+        pass_rest(q)
+    nk = len(MASKS)
+
+    def to_x(r, a, k=0, n=nk):
+        ssem, rsem = (x_send, x_recv) if k else (g_send.at[r % SLOTS, a], g_recv.at[r, a])
+        at = pl.ds(k, n)
+        return remote(theirs.at[r % SLOTS, a, at], arrived.at[r, a, at], ssem, rsem, other_x)
+
+    def to_z(r, a, zd, b, at):
+        return remote(
+            mine.at[r, a, at, zd], red.at[a, b * GROUP + r, at], r_send, r_recv.at[b], (zd * 2 + x, mp)
+        )
+
+    def settle(r, a, k=0, n=nk):
+        to_x(r, a, k, n).wait_recv()
+        at = pl.ds(k, n)
+        mine[r, a, at] = (
+            mine[r, a, at].astype(jnp.float32) + arrived[r, a, at].astype(jnp.float32)
+        ).astype(jnp.bfloat16)
+        for dz in (2, 1, 3):
+            to_z(r, a, (z + dz) % nz, z % 2, at).start()
+        pltpu.make_async_copy(mine.at[r, a, at, z], red.at[a, hbase + r, at], rl_sem).start()
+
+    def step(r, a, first=0, n=nk):
+        for k in range(first, first + n):
+            block = flip(r, MASKS[k])
+            if a == 0:
+                value = dot(xall[0, block], dpreh[r], ((0,), (0,)))
+            else:
+                value = dot(acth[r], xall[1, block], ((0,), (0,)))
+            value = value.astype(jnp.bfloat16).reshape(nz, 2, rows, side)
+            low, high = value[:, 0], value[:, 1]
+            mine[r, a, k] = jnp.where(x == 0, low, high)
+            theirs[r % SLOTS, a, k] = jnp.where(x == 0, high, low)
+        to_x(r, a, first, n).start()
 
     @pl.when(heavy)
     def _():
+        def grads(r):
+            for a in range(2):
+                @pl.when(r >= SLOTS)
+                def _(a=a):
+                    to_x(r - SLOTS, a).wait_send()
+
+                step(r, a)
+
+                @pl.when(r > 0)
+                def _(a=a):
+                    settle(r - 1, a)
+
+        def both_steps(r):
+            loop(HALVES, functools.partial(near, r))
+            grads(r)
+
+        def landed_in(h, n, ssem, rsem):
+            for q in range(h * per, (h + 1) * per):
+                near_part(1 - y, q, 0, n, ssem, rsem).wait_recv()
+
+        for h in range(HALVES):
+            landed_in(h, size(LEAD), fa_send, fa_recv)
+            near(0, h)
+        grads(0)
         release(0)
+        pl.semaphore_signal(go_sem, inc=1, device_id=other_core, device_id_type=MESH)
         emit(0)
-        for q in range(NQ - 1):
-            near_landed(q)
-            loop(GROUP, functools.partial(near, q))
-        near_landed(NQ - 1)
-        pl.semaphore_signal(go_sem, inc=1, device_id=other_core, device_id_type=MESH)
-        near(NQ - 1, 0)
+        loop(hb, lambda u: place(1, u), hb // 2)
+        for h in range(HALVES):
+            landed_in(h, size(RELAY), fb_send, fb_recv)
+            landed_in(h, BOTH[1], fb_send, b_recv)
+            near(1, h)
+        grads(1)
+        hand_over(1)
+        merge(1)
+        release(1)
+        emit(1)
+        loop(6, both_steps, 2)
+        finish(0)
+        loop(GROUP - 1, both_steps, 6)
+        last = GROUP - 1
+        loop(HALVES, functools.partial(near, last))
+        to_x(last - SLOTS, 0).wait_send()
+        to_x(last - SLOTS, 1).wait_send()
+        step(last, 0)
+        settle(last - 1, 0)
+        step(last, 1, 0, 2)
+        settle(last - 1, 1)
+        step(last, 1, 2, 2)
+        settle(last, 0)
+        settle(last, 1, 0, 2)
+        settle(last, 1, 2, 2)
 
     @pl.when(jnp.logical_not(heavy))
     def _():
-        hidden(1)
-        loop(hb, lambda u: place(1, u))
+        loop(hb, lambda u: place(1, u), hb // 2)
         hand_over(1)
         release(0)
         release(1)
@@ -446,88 +525,18 @@
         emit(0)
         merge(1)
         emit(1)
-
-    def to_x(r, a):
-        return remote(
-            theirs.at[r % SLOTS, a], arrived.at[r, a], g_send.at[r % SLOTS, a], g_recv.at[r, a], other_x
-        )
-
-    def to_z(r, a, zd, b):
-        return remote(
-            mine.at[r, a, :, zd], red.at[a, b * GROUP + r],
-            r_send, r_recv.at[b], (zd * 2 + x, mp),
-        )
-
-    def keep_z(r, a):
-        return pltpu.make_async_copy(mine.at[r, a, :, z], red.at[a, hbase + r], rl_sem)
-
-    def settle(r, a):
-        to_x(r, a).wait_recv()
-        mine[r, a] = (
-            mine[r, a].astype(jnp.float32) + arrived[r, a].astype(jnp.float32)
-        ).astype(jnp.bfloat16)
-        for dz in (2, 1, 3):
-            to_z(r, a, (z + dz) % nz, z % 2).start()
-        keep_z(r, a).start()
-
-    @pl.when(heavy)
-    def _():
-        def grads(r, stage=3):
-            for a in range(2):
-                @pl.when(r >= SLOTS)
-                def _(a=a):
-                    to_x(r - SLOTS, a).wait_send()
-
-                for k, m in enumerate(MASKS):
-                    if a == 0:
-                        value = dot(xall[0, flip(r, m)], dpreh[r], ((0,), (0,)))
-                    else:
-                        value = dot(acth[r], xall[1, flip(r, m)], ((0,), (0,)))
-                    value = value.astype(jnp.bfloat16).reshape(nz, 2, rows, side)
-                    low, high = value[:, 0], value[:, 1]
-                    mine[r, a, k] = jnp.where(x == 0, low, high)
-                    theirs[r % SLOTS, a, k] = jnp.where(x == 0, high, low)
-                to_x(r, a).start()
-
-                if stage == 0 and a == 1:
-                    loop(GROUP, functools.partial(near, NQ - 1), 1)
-                if stage == 1:
-                    first = GROUP - hbase + a * (GROUP // 2)
-                    hidden(1, first, first + GROUP // 2)
-                if stage == 2:
-                    step = 2 * (r - 2) + a
-                    loop((step + 1) * (hb // 4), lambda u: place(1, u), step * (hb // 4))
-
-                @pl.when(r > 0)
-                def _(a=a):
-                    settle(r - 1, a)
-
-        grads(0, 0)
-        grads(1, 1)
-        loop(4, functools.partial(grads, stage=2), 2)
-        hand_over(1)
-        release(1)
-        loop(5, grads, 4)
-        merge(1)
-        emit(1)
-        loop(6, grads, 5)
         finish(0)
-        loop(GROUP, grads, 6)
-        settle(GROUP - 1, 0)
-        settle(GROUP - 1, 1)
-
-    @pl.when(jnp.logical_not(heavy))
-    def _():
-        finish(0)
 
     finish(1)
+
     for q in range(NQ):
         for a in range(2):
             swap(a, q).wait_send()
 
         @pl.when(heavy)
         def _(q=q):
-            y_forward(y, q).wait_send()
+            near_part(y, q, 0, size(LEAD), fa_send, fa_recv).wait_send()
+            near_part(y, q, 0, size(RELAY), fb_send, fb_recv).wait_send()
 
     remote(crecv.at[0], crecv.at[0], p_send, p_recv.at[0], other_y).wait_send()
     pltpu.make_async_copy(crecv.at[0], crecv.at[0], out_sem).wait()
@@ -536,7 +545,10 @@
     def _():
         for r in range(GROUP - SLOTS, GROUP):
             for a in range(2):
-                to_x(r, a).wait_send()
+                if a == 0 or r < GROUP - 1:
+                    to_x(r, a).wait_send()
+        to_x(GROUP - 1, 1, 0, 2).wait_send()
+        to_x(GROUP - 1, 1, 2, 2).wait_send()
         group = red.at[:, pl.ds(hbase, GROUP)]
         pltpu.make_async_copy(group, group, rl_sem).wait()
         sent = mine.at[pl.ds(0, GROUP * (nz - 1) // nz)]
@@ -628,13 +640,13 @@
             pltpu.VMEM((2, hb, kk, side, side), bf),
             pltpu.VMEM((2, hb, tok, side), bf),
         ]
-        + [dma((2, NQ))] * 9
-        + [dma((NQ,))] * 4
+        + [dma((2, NQ))] * 10
+        + [dma((NQ,))] * 7
         + [pltpu.SemaphoreType.REGULAR, dma((2,)), pltpu.SemaphoreType.REGULAR((2,))]
         + [dma((2, NQ))] * 2
         + [dma, dma((2,)), dma]
         + [dma((SLOTS, 2)), dma((GROUP, 2))]
-        + [dma, dma((2,)), dma],
+        + [dma, dma, dma, dma((2,)), dma],
         compiler_params=pltpu.CompilerParams(
             collective_id=0, has_side_effects=True, vmem_limit_bytes=67_000_000
         ),

time: 140 us -> 135 us (0.964)
  Pallas kernels: 137 us -> 131 us
    pallas_call x1, Pallas kernels: 133 us -> 127 us  [shards_fused(): pl.pallas_call(functools.partial(fused_kernel, (ndp, nmp, hb, side, own,...]
where the time goes in v5:
time: 135 us; the launch traced here: 133 us
  Pallas kernels  131 us (97%)
    pallas_call x1, Pallas kernels, shards_fused(): pl.pallas_call(functools.partial(fused_kernel, (ndp, nmp, hb, side, own,...  127 us
    pallas_call x1, Pallas kernels, shards_fused(): pl.pallas_call(functools.partial(write_kernel, scale), out_shape=(jax.Sha...  3.97 us

profile of v5, /device:TPU:0, one launch (start us, length us, event | category | flops | bytes accessed | tf_op | source)
XLA Modules:
  0.0 133.3 jit_solution(5657087875641162563)
XLA Ops:
  0.6 0.7 slice_bitcast_fusion
  1.3 0.1 select_reduce_fusion
  1.4 0.6 pad_add_fusion.1.idx
  2.1 127.1 %shard_map.93 = (bf16[256,2048]{1,0:T(8,128)(2,1)}, bf16[256,2048]{1,0:T(8,128)(2,1)}, bf16[2,16,4,32,256]{4,3,2,1,0:T(8,128)(2,1)}) custom-call(s32[2,48]{1,0:T(2,128)} %pad_add_fusion.1.idx, bf16[256,2048]{1,0:T(8,128)(2,1)} %x_hbm.1, bf16[256,2048]{1,0:T(8,128)(2,1)} %dy_hbm.1, bf16[16,4,256,256]{3,2,1,0:T(8,128)(2,1)} %win_hbm.1, ...), custom_call_target="tpu_custom_call" | custom-call | tf_op jit(solution)/shard_map/pallas_call | solution.py:620
  129.2 4.0 %shard_map.94 = (bf16[256,2048]{1,0:T(8,128)(2,1)}, bf16[256,2048]{1,0:T(8,128)(2,1)}, f32[16,4,32,256]{3,2,1,0:T(8,128)}, f32[16,4,32,256]{3,2,1,0:T(8,128)}) custom-call(bf16[256,2048]{1,0:T(8,128)(2,1)} %get-tuple-element.7.out_hbm, bf16[256,2048]{1,0:T(8,128)(2,1)} %get-tuple-element.8.back_hbm, bf16[2,16,4,32,256]{4,3,2,1,0:T(8,128)(2,1)} %get-tuple-element.9.red), custom_call_target="tpu_custom_call" | custom-call | tf_op jit(solution)/shard_map/pallas_call | solution.py:659
  (1 shorter events, 0.0 us)

commit v6 on v5

--- a/solution.py
+++ b/solution.py
@@ -17,8 +17,8 @@
 NQ = 4
 LEAD = ((0, 3), (4, 1))
 REST = ((3, 1), (5, 3))
-RELAY = ((3, 1),)
-BOTH = (5, 3)
+RELAYS = (((3, 1),), ((3, 1),), ((3, 1), (5, 1)), ((3, 1), (5, 1)))
+BOTHS = ((5, 3), (5, 3), (6, 2), (6, 2))
 SLOTS = 4
 PIECES = 4
 HALVES = 2
@@ -250,7 +250,7 @@
         pass_on(q, LEAD, za_recv, fa_send, fa_recv, LEAD)
 
     def pass_rest(q):
-        pass_on(q, RELAY, zb_recv, fb_send, fb_recv, REST)
+        pass_on(q, RELAYS[q], zb_recv, fb_send, fb_recv, REST)
 
     def gather(a, q):
         landed(to_y, a, q, g_y).wait_recv()
@@ -295,17 +295,16 @@
 
         loop(last, one, first)
 
-    def place(h, u):
-        at = pl.ds(h * ht, ht)
+    def place(u):
         vs = [flip(u, m) for m in MASKS]
         wo = jnp.concatenate([wall[1, v, k] for k, v in enumerate(vs)], axis=0)
         wi = jnp.concatenate([wall[0, v, k] for k, v in enumerate(vs)], axis=1)
-        out = dot(jnp.concatenate([act[v, at] for v in vs], axis=1), wo, ((1,), (0,)))
-        back = dot(jnp.concatenate([dpre[v, at] for v in vs], axis=1), wi, ((1,), (1,)))
+        out = dot(jnp.concatenate([act[v] for v in vs], axis=1), wo, ((1,), (0,)))
+        back = dot(jnp.concatenate([dpre[v] for v in vs], axis=1), wi, ((1,), (1,)))
         for a, value in ((0, out), (1, back)):
             value = value.astype(jnp.bfloat16)
-            for p in range(per):
-                fulls[a][h * per + p][u] = value[p * tc : (p + 1) * tc]
+            for q in range(NQ):
+                fulls[a][q][u] = value[q * tc : (q + 1) * tc]
 
     tables = (1, 0)
 
@@ -334,10 +333,11 @@
                     loop(own, fill)
                 swap(a, q).start()
 
-    def to_part(a, h, i):
+    def to_part(a, h):
         at = pl.ds(h * ht, ht)
         return remote(
-            crecv.at[a, (1 - y) * own + i, at], xg.at[a, i, at], p_send, p_recv.at[h], other_y
+            crecv.at[a, pl.ds((1 - y) * own, own), at], xg.at[a, pl.ds(0, own), at],
+            p_send, p_recv.at[h], other_y,
         )
 
     def put(a, h, i):
@@ -372,7 +372,7 @@
     def emit(h):
         pl.semaphore_wait(free_sem.at[h], 1)
         for a in range(2):
-            loop(own, lambda i, a=a: to_part(a, h, i).start())
+            to_part(a, h).start()
 
     def near(r, p):
         at = pl.ds(pl.multiple_of(p * per * nz * tc, per * nz * tc), per * nz * tc)
@@ -387,7 +387,7 @@
                 def _(b=b, q=q):
                     z_sent(y, b, q, size(LEAD), za_send, za_recv)
                     z_sent(y, b, q, size(REST), zb_send, zb_recv)
-                    z_sent(1 - y, b, q, BOTH[1], b_send, b_recv)
+                    z_sent(1 - y, b, q, BOTHS[q][1], b_send, b_recv)
 
         pl.semaphore_signal(free_sem.at[h], inc=1, device_id=other_y, device_id_type=MESH)
 
@@ -408,23 +408,23 @@
             def _(a=a, q=q):
                 gather(a, q)
 
-        to_groups(1 - y, q, (BOTH,), b_send, b_recv)
+        to_groups(1 - y, q, (BOTHS[q],), b_send, b_recv)
         if q == per - 1:
             hidden(0)
         if q == per:
             pass_lead(0)
             pass_lead(1)
-            clear(0)
-            loop(hb, lambda u: place(0, u))
     for q in range(per, NQ):
         pass_lead(q)
+    hidden(1)
+    clear(0)
+    clear(1)
+    loop(hb, place)
     hand_over(0)
-    hidden(1)
-    clear(1)
-    merge(0)
-    loop(hb // 2, lambda u: place(1, u))
+    hand_over(1)
     for q in range(NQ):
         pass_rest(q)
+
     nk = len(MASKS)
 
     def to_x(r, a, k=0, n=nk):
@@ -478,27 +478,26 @@
             loop(HALVES, functools.partial(near, r))
             grads(r)
 
-        def landed_in(h, n, ssem, rsem):
+        def landed_in(h, counts, ssem, rsem):
             for q in range(h * per, (h + 1) * per):
-                near_part(1 - y, q, 0, n, ssem, rsem).wait_recv()
+                near_part(1 - y, q, 0, counts[q], ssem, rsem).wait_recv()
 
         for h in range(HALVES):
-            landed_in(h, size(LEAD), fa_send, fa_recv)
+            landed_in(h, [size(LEAD)] * NQ, fa_send, fa_recv)
             near(0, h)
         grads(0)
         release(0)
+        release(1)
+        merge(0)
+        merge(1)
         pl.semaphore_signal(go_sem, inc=1, device_id=other_core, device_id_type=MESH)
         emit(0)
-        loop(hb, lambda u: place(1, u), hb // 2)
+        emit(1)
         for h in range(HALVES):
-            landed_in(h, size(RELAY), fb_send, fb_recv)
-            landed_in(h, BOTH[1], fb_send, b_recv)
+            landed_in(h, [size(spans) for spans in RELAYS], fb_send, fb_recv)
+            landed_in(h, [n for _, n in BOTHS], fb_send, b_recv)
             near(1, h)
         grads(1)
-        hand_over(1)
-        merge(1)
-        release(1)
-        emit(1)
         loop(6, both_steps, 2)
         finish(0)
         loop(GROUP - 1, both_steps, 6)
@@ -517,13 +516,12 @@
 
     @pl.when(jnp.logical_not(heavy))
     def _():
-        loop(hb, lambda u: place(1, u), hb // 2)
-        hand_over(1)
         release(0)
         release(1)
+        merge(0)
+        merge(1)
         pl.semaphore_wait(go_sem, 1)
         emit(0)
-        merge(1)
         emit(1)
         finish(0)
 
@@ -536,7 +534,7 @@
         @pl.when(heavy)
         def _(q=q):
             near_part(y, q, 0, size(LEAD), fa_send, fa_recv).wait_send()
-            near_part(y, q, 0, size(RELAY), fb_send, fb_recv).wait_send()
+            near_part(y, q, 0, size(RELAYS[q]), fb_send, fb_recv).wait_send()
 
     remote(crecv.at[0], crecv.at[0], p_send, p_recv.at[0], other_y).wait_send()
     pltpu.make_async_copy(crecv.at[0], crecv.at[0], out_sem).wait()

time: 135 us -> 132 us (0.978)
  Pallas kernels: 131 us -> 129 us
    pallas_call x1, Pallas kernels: 127 us -> 125 us  [shards_fused(): pl.pallas_call(functools.partial(fused_kernel, (ndp, nmp, hb, side, own,...]
where the time goes in v6:
time: 132 us; the launch traced here: 131 us
  Pallas kernels  129 us (98%)
    pallas_call x1, Pallas kernels, shards_fused(): pl.pallas_call(functools.partial(fused_kernel, (ndp, nmp, hb, side, own,...  125 us
    pallas_call x1, Pallas kernels, shards_fused(): pl.pallas_call(functools.partial(write_kernel, scale), out_shape=(jax.Sha...  3.97 us

profile of v6, /device:TPU:0, one launch (start us, length us, event | category | flops | bytes accessed | tf_op | source)
XLA Modules:
  0.0 131.1 jit_solution(6548686735753559399)
XLA Ops:
  0.6 0.7 slice_bitcast_fusion
  1.3 0.1 select_reduce_fusion
  1.4 0.6 pad_add_fusion.1.idx
  2.1 124.9 %shard_map.93 = (bf16[256,2048]{1,0:T(8,128)(2,1)}, bf16[256,2048]{1,0:T(8,128)(2,1)}, bf16[2,16,4,32,256]{4,3,2,1,0:T(8,128)(2,1)}) custom-call(s32[2,48]{1,0:T(2,128)} %pad_add_fusion.1.idx, bf16[256,2048]{1,0:T(8,128)(2,1)} %x_hbm.1, bf16[256,2048]{1,0:T(8,128)(2,1)} %dy_hbm.1, bf16[16,4,256,256]{3,2,1,0:T(8,128)(2,1)} %win_hbm.1, ...), custom_call_target="tpu_custom_call" | custom-call | tf_op jit(solution)/shard_map/pallas_call | solution.py:618
  127.0 4.0 %shard_map.94 = (bf16[256,2048]{1,0:T(8,128)(2,1)}, bf16[256,2048]{1,0:T(8,128)(2,1)}, f32[16,4,32,256]{3,2,1,0:T(8,128)}, f32[16,4,32,256]{3,2,1,0:T(8,128)}) custom-call(bf16[256,2048]{1,0:T(8,128)(2,1)} %get-tuple-element.7.out_hbm, bf16[256,2048]{1,0:T(8,128)(2,1)} %get-tuple-element.8.back_hbm, bf16[2,16,4,32,256]{4,3,2,1,0:T(8,128)(2,1)} %get-tuple-element.9.red), custom_call_target="tpu_custom_call" | custom-call | tf_op jit(solution)/shard_map/pallas_call | solution.py:657
  (1 shorter events, 0.0 us)
